TPU v7x, 32 devices: a whole 2x2x4 slice. The times are simulated.
32 devices in a mesh: dp: 2 (over core), row: 4 (over y, x), col: 4 (over z).
Axes of the slice: x: 2, y: 2, z: 4, core: 2. Of those that a mesh axis runs over, the one named last changes fastest.
Arguments:
- inputs: bfloat16 [32768, 768], P(('dp', 'row', 'col')), may hold values from -6 to 6
- segment_ids: int32 [32768], P(('dp', 'row', 'col')), may hold values from 0 to 3, as said below
- query_weight: bfloat16 [768, 768], P('row', 'col'), may hold values from -0.21875 to 0.21875
- key_weight: bfloat16 [768, 768], P('row', 'col'), may hold values from -0.21875 to 0.21875
- value_weight: bfloat16 [768, 768], P('row', 'col'), may hold values from -0.21875 to 0.21875
- output_weight: bfloat16 [768, 768], P('row', 'col'), may hold values from -1.75 to 1.75
- gate_weight: bfloat16 [768, 2048], P('row', 'col'), may hold values from -0.21875 to 0.21875
- up_weight: bfloat16 [768, 2048], P('row', 'col'), may hold values from -0.21875 to 0.21875
- down_weight: bfloat16 [2048, 768], P('row', 'col'), may hold values from -0.125 to 0.125
- first_gain: bfloat16 [768], P(('row', 'col')), may hold values from 0.099609375 to 1.8984375
- second_gain: bfloat16 [768], P(('row', 'col')), may hold values from 0.099609375 to 1.8984375
- cotangent: bfloat16 [32768, 768], P(('dp', 'row', 'col')), may hold values from -6 to 6
Outputs:
- layer_out: bfloat16 [32768, 768], P(('dp', 'row', 'col'))
- input_grad: bfloat16 [32768, 768], P(('dp', 'row', 'col'))
- query_grad: float32 [768, 768], P('row', 'col')
- key_grad: float32 [768, 768], P('row', 'col')
- value_grad: float32 [768, 768], P('row', 'col')
- output_grad: float32 [768, 768], P('row', 'col')
- gate_grad: float32 [768, 2048], P('row', 'col')
- up_grad: float32 [768, 2048], P('row', 'col')
- down_grad: float32 [2048, 768], P('row', 'col')
- first_gain_grad: float32 [768], P(('row', 'col'))
- second_gain_grad: float32 [768], P(('row', 'col'))
Inputs may be any that keep to these rules, and one draw needn't show every extreme that they name: `segment_ids`: within each aligned block of 1024 tokens the ids number that block's sequences 0, 1, ... in order; a block holds 1, 2 or 4 sequences of equal length, and each of the three cases occurs in some block.
All inputs are finite; a program needn't handle non-finite values.
Results may differ from a plain program's by a relative error of at most 0.017.
Values may be sent and summed in bfloat16 or wider, within the bound.
No kernel may reach another device: no remote copies, remote signals or barrier semaphores. Data moves between devices by JAX's collectives and lax.ppermute only.
A program may use at most 192 MiB of HBM per device.

v0:
```python
import jax
import jax.numpy as jnp
from jax import lax
from jax.experimental import pallas as pl
from jax.experimental.pallas import tpu as pltpu
from jax.sharding import PartitionSpec as P

HEAD_DIM = 64
EPSILON = 1e-06
ROPE_BASE = 10000.0
NEGATIVE = -1e30
LOG2E = 1.4426950408889634
QUERY_BLOCK = 256
LANES = 128
BF16 = jnp.bfloat16
F32 = jnp.float32
EVERYWHERE = ("dp", "row", "col")


def costs(microseconds):
    return pl.CostEstimate(flops=int(microseconds * 1e7), bytes_accessed=int(microseconds * 1e4), transcendentals=0)


def dot_nn(left, right):
    return lax.dot_general(left, right, (((1,), (0,)), ((), ())), preferred_element_type=F32)


def dot_nt(left, right):
    return lax.dot_general(left, right, (((1,), (1,)), ((), ())), preferred_element_type=F32)


def bit_count(size):
    return size.bit_length() - 1


def bit_order(grid_rows, grid_cols, core):
    col_bits = [("col", b) for b in range(bit_count(grid_cols))]
    row_bits = [("row", b) for b in range(bit_count(grid_rows))]
    return (col_bits[::-1] + row_bits[::-1]) if core else (col_bits + row_bits)


def step_pairs(grid_rows, grid_cols, step):
    pairs = []
    for core in range(2):
        axis, bit = bit_order(grid_rows, grid_cols, core)[step]
        for row in range(grid_rows):
            for col in range(grid_cols):
                to_row = row ^ (1 << bit) if axis == "row" else row
                to_col = col ^ (1 << bit) if axis == "col" else col
                source = (core * grid_rows + row) * grid_cols + col
                target = (core * grid_rows + to_row) * grid_cols + to_col
                pairs.append((source, target))
    return pairs


def other_core(value):
    return lax.ppermute(value, "dp", [(0, 1), (1, 0)])


def exchange(value, grid, step):
    return lax.ppermute(value, EVERYWHERE, step_pairs(*grid, step))


def tie(*values):
    return lax.optimization_barrier(values)


def sum_blocks_body(shape, *refs):
    parts, came = shape
    out = refs[-1]
    came_refs = refs[len(refs) - 1 - came : -1]
    at = begin = 0
    for count in parts:
        end = begin + refs[at].shape[2]
        total = sum(ref[...].astype(F32) for ref in refs[at : at + count])
        for ref in came_refs:
            total = total + ref[:, :, begin:end, :].astype(F32)
        out[:, :, begin:end, :] = total.astype(BF16)
        at += count
        begin = end


class Scatter:
    def __init__(self, grid):
        self.grid = grid
        self.parts = []
        self.came = []

    def add(self, *terms):
        self.parts.append(list(terms))

    def put(self, came, origin=(0, 0)):
        self.came.append((came, origin))

    def terms(self, start, size):
        came = []
        for value, origin in self.came:
            inside = [o <= a and a + n <= o + m for o, a, n, m in zip(origin, start, size, value.shape)]
            apart = [a + n <= o or o + m <= a for o, a, n, m in zip(origin, start, size, value.shape)]
            assert all(inside) or any(apart)
            if all(inside):
                came.append((value, origin))
        return [(term, (0, 0)) for part in self.parts for term in part], came

    def sums(self, start, size):
        height = sum(part[0].shape[2] for part in self.parts)
        width = self.parts[0][0].shape[3]
        parts, came = self.terms(start, size)
        terms = parts + came
        if len(self.parts) == 1:
            values = []
            for term, origin in terms:
                begin = [a - o for a, o in zip(start, origin)]
                values.append(term[begin[0] : begin[0] + size[0], begin[1] : begin[1] + size[1]])
            if len(values) == 2:
                return values[0] + values[1]
            return sum(value.astype(F32) for value in values).astype(BF16)
        axis = 0 if size[0] > 1 else 1
        count = 2 if size[axis] > 1 else 1
        block = list(size)
        block[axis] //= count

        def spec(rows, begin):
            first = begin[0] // block[0], begin[1] // block[1]
            step = (lambda i: (first[0] + i, first[1], 0, 0)) if axis == 0 else (lambda i: (first[0], first[1] + i, 0, 0))
            return pl.BlockSpec((block[0], block[1], rows, width), step)

        return pl.pallas_call(
            lambda *refs: sum_blocks_body(([len(part) for part in self.parts], len(came)), *refs),
            grid=(count,),
            in_specs=[spec(term.shape[2], [a - o for a, o in zip(start, origin)]) for term, origin in terms],
            out_specs=spec(height, (0, 0)),
            out_shape=jax.ShapeDtypeStruct((size[0], size[1], height, width), BF16),
            cost_estimate=costs(2),
            name="sum_blocks",
        )(*[term for term, _ in terms])

    def send(self, value, step):
        return exchange(value, self.grid, step)


def last_sums_body(shapes, *refs):
    out = refs[-1]
    at = top = 0
    for parts, came in shapes:
        count = sum(parts) + came
        group = refs[at : at + count]
        height = sum(group[sum(parts[:k])].shape[2] for k in range(len(parts)))
        width = group[0].shape[3]
        begin = first = 0
        for n in parts:
            end = begin + group[first].shape[2]
            total = sum(ref[0, 0].astype(F32) for ref in group[first : first + n])
            for ref in group[count - came :]:
                total = total + ref[0, 0, begin:end, :].astype(F32)
            out[top + begin : top + end, 0:width] = total.astype(BF16)
            first += n
            begin = end
        top += height
        at += count


def last_sums(scatters):
    shapes, terms, height, width = [], [], 0, 0
    for scatter in scatters:
        parts, came = scatter.terms([0, 0], [1, 1])
        shapes.append(([len(part) for part in scatter.parts], len(came)))
        terms += parts + came
        height += sum(part[0].shape[2] for part in scatter.parts)
        width = max(width, scatter.parts[0][0].shape[3])

    def spec(term, origin):
        return pl.BlockSpec((1, 1, *term.shape[2:]), lambda i: (-origin[0], -origin[1], 0, 0))

    return pl.pallas_call(
        lambda *refs: last_sums_body(shapes, *refs),
        grid=(1,),
        in_specs=[spec(*term) for term in terms],
        out_specs=pl.BlockSpec((height, width), lambda i: (0, 0)),
        out_shape=jax.ShapeDtypeStruct((height, width), BF16),
        cost_estimate=costs(2),
        name="last_sums",
    )(*[term for term, _ in terms])


def reversed_bits(value, bits):
    out = 0
    for b in range(bits):
        out = out | (((value >> b) & 1) << (bits - 1 - b))
    return out


def place_of(row, col, place, core, grid_rows, grid_cols):
    far_row = row ^ place[0]
    far_col = col ^ place[1]
    row_bits = bit_count(grid_rows)
    col_bits = bit_count(grid_cols)
    plain = far_col + far_row * grid_cols
    turned = reversed_bits(far_col, col_bits) + reversed_bits(far_row, row_bits) * grid_cols
    return jnp.where(core == 0, plain, turned)


def unpack_pair(packed, odd):
    firsts = []
    for k in range(2):
        body = packed[:, 128 * k : 128 * (k + 1)]
        rest_low, rest_high = packed[:, 256:320], packed[:, 320:384]
        in_order, turned = (rest_low, rest_high) if k == 0 else (rest_high, rest_low)
        plain = jnp.concatenate([body, in_order], axis=1)
        other = jnp.concatenate([turned, body], axis=1)
        firsts.append(jnp.where(odd, other, plain))
    return firsts


def by_core(place, mine, theirs):
    mine, theirs = mine.astype(F32), theirs.astype(F32)
    first = place[2] == 0
    return jnp.where(first, mine, theirs), jnp.where(first, theirs, mine)


def finish_body(place, mine, theirs, query, key, value, output, gate, up, down, gain_one, gain_two):
    half = down.shape[0] // 2
    quarter = half // 2
    share = gain_one.shape[0]
    odd = (place[1] & 1) == 1
    halves = by_core(place, mine[...], theirs[...])
    for core, part in enumerate(halves):
        rows = slice(core * half, (core + 1) * half)
        for k, out in enumerate((gate, up, down)):
            out[rows, :] = part[k * half : (k + 1) * half]
        low = 3 * half + quarter
        query[rows, :], key[rows, :] = unpack_pair(part[low : low + half, :384], odd)
        for out, begin in ((output, 3 * half), (value, low + half)):
            for k, block in enumerate(unpack_pair(part[begin : begin + quarter, :384], odd)):
                out[core * half + k * quarter : core * half + (k + 1) * quarter, :] = block
    gains = halves[0][3 * half : 3 * half + 8, 384:512]
    gain_one[...] = gains[0, :share]
    gain_two[...] = gains[1, :share]


def finish(place, mine, theirs, shapes):
    vmem = pl.BlockSpec(memory_space=pltpu.VMEM)
    return pl.pallas_call(
        finish_body,
        in_specs=[pl.BlockSpec(memory_space=pltpu.SMEM)] + [vmem] * 2,
        out_specs=[vmem] * len(shapes),
        out_shape=[jax.ShapeDtypeStruct(shape, F32) for shape in shapes],
        cost_estimate=costs(1),
        name="finish",
    )(place, mine, theirs)


def pack_pair(first, second, odd, out, rows):
    rolled = [jnp.concatenate([v[:, 64:], v[:, :64]], axis=1) for v in (first, second)]
    bodies = [jnp.where(odd, r[:, :128], v[:, :128]) for r, v in zip(rolled, (first, second))]
    rests = [jnp.where(odd, v[:, :64], v[:, 128:]) for v in (first, second)]
    low = jnp.where(odd, rests[1], rests[0])
    high = jnp.where(odd, rests[0], rests[1])
    out[rows, 0:128] = bodies[0].astype(BF16)
    out[rows, 128:256] = bodies[1].astype(BF16)
    out[rows, 256:384] = jnp.concatenate([low, high], axis=1).astype(BF16)


def pack_attention_body(place, query, key, value, out):
    half = query.shape[0] // 2
    quarter = half // 2
    odd = (place[1] & 1) == 1
    base = place[2] * half
    query, key = (w[pl.ds(pl.multiple_of(base, half), half), :].astype(F32) for w in (query, key))
    pack_pair(query, key, odd, out, slice(0, half))
    value = value[pl.ds(pl.multiple_of(base, half), half), :].astype(F32)
    pack_pair(value[:quarter], value[quarter:], odd, out, slice(half, half + quarter))


def pack_attention(place, query, key, value):
    half = query.shape[0] // 2
    vmem = pl.BlockSpec(memory_space=pltpu.VMEM)
    return pl.pallas_call(
        pack_attention_body,
        in_specs=[pl.BlockSpec(memory_space=pltpu.SMEM)] + [vmem] * 3,
        out_specs=vmem,
        out_shape=jax.ShapeDtypeStruct((half + half // 2, 384), BF16),
        cost_estimate=costs(2),
        name="pack_attention",
    )(place, query, key, value)


def pack_feed_body(place, gate, up, down, output, gain_one, gain_two, out):
    half = gate.shape[0] // 2
    quarter = half // 2
    odd = (place[1] & 1) == 1
    rows = pl.ds(pl.multiple_of(place[2] * half, half), half)
    out[0:half, :] = gate[rows, :]
    out[half : 2 * half, :] = up[rows, :]
    out[2 * half + quarter : 3 * half + quarter, :] = down[rows, :]
    output = output[rows, :].astype(F32)
    low = slice(2 * half, 2 * half + quarter)
    pack_pair(output[:quarter], output[quarter:], odd, out, low)
    share = gain_one.shape[1]
    gains = jnp.concatenate([gain_one[...].astype(F32), gain_two[...].astype(F32)], axis=0)
    gains = jnp.concatenate([gains, jnp.zeros((2, LANES - share), F32)], axis=1)
    gains = jnp.concatenate([gains, jnp.zeros((quarter - 2, LANES), F32)], axis=0)
    out[low, 384:512] = gains.astype(BF16)


def pack_feed(place, gate, up, down_turned, output, gain_one, gain_two):
    half = gate.shape[0] // 2
    vmem = pl.BlockSpec(memory_space=pltpu.VMEM)
    return pl.pallas_call(
        pack_feed_body,
        in_specs=[pl.BlockSpec(memory_space=pltpu.SMEM)] + [vmem] * 6,
        out_specs=vmem,
        out_shape=jax.ShapeDtypeStruct((3 * half + half // 2, gate.shape[1]), BF16),
        cost_estimate=costs(2),
        name="pack_feed",
    )(place, gate, up, down_turned, output, gain_one[None], gain_two[None])


def place_scalars():
    return jnp.stack([lax.axis_index("row"), lax.axis_index("col"), lax.axis_index("dp")]).astype(jnp.int32)


def split_rows(top):
    return lax.broadcasted_iota(jnp.int32, top, 1) < 64


def fill_columns(target, rows, low_even, body_even, low_odd, body_odd, pair, swapped):
    base = 384 * pair
    target[rows, base : base + 128] = body_even
    target[rows, base + 256 : base + 384] = body_odd
    first = split_rows(low_even.shape)
    if swapped:
        mixed = jnp.where(first, low_odd, low_even)
        target[rows, base + 128 : base + 256] = pltpu.roll(mixed.astype(F32), 64, 1).astype(BF16)
    else:
        target[rows, base + 128 : base + 256] = jnp.where(first, low_even, low_odd)


def piece_places(pieces):
    counts = [p.shape[0] for p in pieces]
    out = []
    for side in range(2):
        at = 0
        for count in counts[side * len(counts) // 2 : (side + 1) * len(counts) // 2]:
            out.append((side, at, count))
            at += count
    return out


def load_stacks(pieces, held, sems):
    copies = []
    for k, (piece, (side, at, count)) in enumerate(zip(pieces, piece_places(pieces))):
        copies.append(pltpu.make_async_copy(piece, held.at[side, pl.ds(at, count)], sems.at[k]))
    for copy in copies:
        copy.start()
    for copy in copies:
        copy.wait()


def assemble_attention(grid, place, held, w_query, w_key, w_value):
    grid_rows, grid_cols = grid
    where = (place[0], place[1])
    half = w_query.shape[0] // grid_rows // 2
    quarter = half // 2
    for core in range(2):
        side = core ^ place[2]
        for row in range(grid_rows):
            start = row * 2 * half + core * half
            for pair in range(grid_cols // 2):
                at = [place_of(row, 2 * pair + c, where, core, grid_rows, grid_cols) for c in range(2)]
                even, odd = (held.at[side, p] for p in at)
                top = slice(0, half)
                rows = slice(start, start + half)
                rest_even, rest_odd = even[top, 256:384], odd[top, 256:384]
                fill_columns(w_query, rows, rest_even, even[top, 0:128], rest_odd, odd[top, 0:128], pair, False)
                fill_columns(w_key, rows, rest_even, even[top, 128:256], rest_odd, odd[top, 128:256], pair, True)
                low = slice(half, half + quarter)
                rest_even, rest_odd = even[low, 256:384], odd[low, 256:384]
                rows = slice(start, start + quarter)
                fill_columns(w_value, rows, rest_even, even[low, 0:128], rest_odd, odd[low, 0:128], pair, False)
                rows = slice(start + quarter, start + half)
                fill_columns(w_value, rows, rest_even, even[low, 128:256], rest_odd, odd[low, 128:256], pair, True)


def assemble_output(grid, place, held, w_output, gains):
    grid_rows, grid_cols = grid
    where = (place[0], place[1])
    half = w_output.shape[0] // grid_rows // 2
    quarter = half // 2
    width = gains.shape[1]
    share = width // (grid_rows * grid_cols)
    lane = lax.broadcasted_iota(jnp.int32, (LANES, width), 1)
    spread = (lax.rem(lane, share) == lax.broadcasted_iota(jnp.int32, (LANES, width), 0)).astype(BF16)
    block_of = lax.div(lax.broadcasted_iota(jnp.int32, (16, width), 1), share)
    total = jnp.zeros((16, width), F32)
    every = slice(0, quarter)
    for core in range(2):
        side = core ^ place[2]
        for row in range(grid_rows):
            start = row * 2 * half + core * half
            for pair in range(grid_cols // 2):
                at = [place_of(row, 2 * pair + c, where, core, grid_rows, grid_cols) for c in range(2)]
                even, odd = (held.at[side, p] for p in at)
                rest_even, rest_odd = even[every, 256:384], odd[every, 256:384]
                rows = slice(start, start + quarter)
                fill_columns(w_output, rows, rest_even, even[every, 0:128], rest_odd, odd[every, 0:128], pair, False)
                rows = slice(start + quarter, start + half)
                fill_columns(w_output, rows, rest_even, even[every, 128:256], rest_odd, odd[every, 128:256], pair, True)
                if core == 0:
                    for c, block in enumerate((even, odd)):
                        spreaded = dot_nn(block[0:16, 384:512], spread)
                        total = total + jnp.where(block_of == row * grid_cols + 2 * pair + c, spreaded, 0.0)
    gains[...] = total[:8]


def block_at(position, place, core, grid):
    grid_rows, grid_cols = grid
    far_row, far_col = position // grid_cols, position % grid_cols
    turned_row, turned_col = reversed_bits(far_row, bit_count(grid_rows)), reversed_bits(far_col, bit_count(grid_cols))
    first = core == 0
    return jnp.where(first, far_row, turned_row) ^ place[0], jnp.where(first, far_col, turned_col) ^ place[1]


def start_feed_copies(grid, place, pieces, w_gate, w_up, w_down, held, sems):
    grid_rows, grid_cols = grid
    half = w_gate.shape[0] // grid_rows // 2
    quarter = half // 2
    span = w_gate.shape[1] // grid_cols
    for piece, (side, at, count) in zip(pieces, piece_places(pieces)):
        core = side ^ place[2]

        @pl.loop(0, count)
        def _(n):
            row, col = block_at(at + n, place, core, grid)
            block = piece.at[n]
            rows = pl.ds(pl.multiple_of((2 * row + core) * half, half), half)
            lanes = pl.ds(pl.multiple_of(col * span, span), span)
            turned_rows = pl.ds(pl.multiple_of((2 * col + core) * half, half), half)
            turned_lanes = pl.ds(pl.multiple_of(row * span, span), span)
            parts = (
                (0, 2 * half, quarter, held.at[side, at + n]),
                (1, 0, half, w_gate.at[rows, lanes]),
                (2, half, half, w_up.at[rows, lanes]),
                (3, 2 * half + quarter, half, w_down.at[turned_rows, turned_lanes]),
            )
            for k, start, size, target in parts:
                pltpu.make_async_copy(block.at[pl.ds(start, size)], target, sems.at[k]).start()


def swap_halves(values):
    lane = lax.broadcasted_iota(jnp.int32, values.shape, 1)
    back = pltpu.roll(values, 32, 1)
    ahead = pltpu.roll(values, LANES - 32, 1)
    return jnp.where(lax.rem(lane, HEAD_DIM) < HEAD_DIM // 2, ahead, back)


def project_tile(x, w_query, w_key, w_value, cosine, sine, query, key, value):
    width = w_query.shape[1]
    step = 256
    for start in range(0, width, step):
        for weight, out in ((w_query, query), (w_key, key)):
            flat = dot_nn(x[...], weight[:, start : start + step])
            for k in range(step // LANES):
                part = flat[:, k * LANES : (k + 1) * LANES]
                turned = part * cosine[...] + swap_halves(part) * sine[...]
                out[:, start + k * LANES : start + (k + 1) * LANES] = turned.astype(BF16)
        value[:, start : start + step] = dot_nn(x[...], w_value[:, start : start + step]).astype(BF16)


def project_blocks_body(grid, count, place, *refs):
    pieces, refs = refs[:count], refs[count:]
    x, cosine, sine, query, key, value, w_query, w_key, w_value, held, sems = refs

    @pl.when(pl.program_id(0) == 0)
    def _():
        load_stacks(pieces, held, sems)
        assemble_attention(grid, place, held, w_query, w_key, w_value)

    project_tile(x, w_query, w_key, w_value, cosine, sine, query, key, value)


def project_blocks(pieces, place, grid, x, cosine, sine):
    tokens, width = x.shape
    _, height, lanes = pieces[0].shape
    rows = 256
    tile = pl.BlockSpec((rows, width), lambda i: (i, 0))
    table = pl.BlockSpec((rows, LANES), lambda i: (i, 0))
    whole = pl.BlockSpec((width, width), lambda i: (0, 0), pipeline_mode=pl.Buffered(1))
    anywhere = pl.BlockSpec(memory_space=pl.ANY)
    return pl.pallas_call(
        lambda *refs: project_blocks_body(grid, len(pieces), *refs),
        grid=(tokens // rows,),
        in_specs=[pl.BlockSpec(memory_space=pltpu.SMEM)] + [anywhere] * len(pieces) + [tile, table, table],
        out_specs=[tile] * 3 + [whole] * 3,
        out_shape=[jax.ShapeDtypeStruct((tokens, width), BF16)] * 3 + [jax.ShapeDtypeStruct((width, width), BF16)] * 3,
        scratch_shapes=[
            pltpu.VMEM((2, grid[0] * grid[1], height, lanes), BF16),
            pltpu.SemaphoreType.DMA((len(pieces),)),
        ],
        cost_estimate=costs(10),
        name="project_heads",
    )(place, *pieces, x, cosine, sine)


def project(x, w_query, w_key, w_value, cosine, sine):
    tokens, width = x.shape
    rows = 256
    tile = pl.BlockSpec((rows, width), lambda i: (i, 0))
    table = pl.BlockSpec((rows, LANES), lambda i: (i, 0))
    whole = pl.BlockSpec((width, width), lambda i: (0, 0))
    return pl.pallas_call(
        project_tile,
        grid=(tokens // rows,),
        in_specs=[tile, whole, whole, whole, table, table],
        out_specs=[tile] * 3,
        out_shape=[jax.ShapeDtypeStruct((tokens, width), BF16)] * 3,
        name="project_heads_plain",
    )(x, w_query, w_key, w_value, cosine, sine)


def own_half(values, h):
    zero = jnp.zeros_like(values)
    return jnp.concatenate([values, zero] if h == 0 else [zero, values], axis=0)


def attention_forward_body(first, q_ref, k_ref, v_ref, context_ref, lse_ref):
    q_turned = (q_ref[...].astype(F32) * HEAD_DIM**-0.5).T.astype(BF16)
    v_turned = v_ref[...].T
    square = (LANES, LANES)
    causal = lax.broadcasted_iota(jnp.int32, square, 0) <= lax.broadcasted_iota(jnp.int32, square, 1)
    lse_ref[...] = jnp.zeros_like(lse_ref)
    for t in range(q_ref.shape[0] // LANES):
        now = slice(t * LANES, (t + 1) * LANES)
        begin = first[t * LANES // QUERY_BLOCK]
        outs = []
        for h in range(2):
            head = slice(h * HEAD_DIM, (h + 1) * HEAD_DIM)
            mine = own_half(q_turned[head, now], h)
            for b in [t, *range(t)]:
                there = slice(b * LANES, (b + 1) * LANES)
                scores = dot_nn(k_ref[there, :], mine)
                if b == t:
                    scores = jnp.where(causal, scores, NEGATIVE)
                block_top = jnp.max(scores, axis=0, keepdims=True) * LOG2E
                if b == t:
                    new_top = base = block_top
                else:
                    seen = begin <= b * LANES // QUERY_BLOCK
                    new_top = jnp.maximum(top, jnp.where(seen, block_top, NEGATIVE))
                    base = new_top + jnp.where(seen, 0.0, -NEGATIVE)
                weights = jnp.exp2(scores * LOG2E - base)
                part_total = jnp.sum(weights, axis=0, keepdims=True)
                part = dot_nn(v_turned[head, there], weights.astype(BF16))
                if b == t:
                    total, mixed = part_total, part
                else:
                    shrink = jnp.exp2(top - new_top)
                    total = total * shrink + part_total
                    mixed = mixed * shrink + part
                top = new_top
            outs.append(mixed * (1.0 / total))
            lse_ref[0, h : h + 1, now] = top + jnp.log2(total)
        context_ref[now, :] = jnp.concatenate(outs, axis=0).T.astype(BF16)


def attention_forward(first, query, key, value, begin, pairs):
    tokens = query.shape[0]
    spec = pl.BlockSpec((tokens, LANES), lambda j, f: (0, j + begin))
    part = pl.BlockSpec((tokens, LANES), lambda j, f: (0, j))
    return pl.pallas_call(
        attention_forward_body,
        grid_spec=pltpu.PrefetchScalarGridSpec(
            num_scalar_prefetch=1,
            grid=(pairs,),
            in_specs=[spec] * 3,
            out_specs=[part, pl.BlockSpec((1, 8, tokens), lambda j, f: (j, 0, 0))],
        ),
        out_shape=[
            jax.ShapeDtypeStruct((tokens, pairs * LANES), BF16),
            jax.ShapeDtypeStruct((pairs, 8, tokens), F32),
        ],
        cost_estimate=costs(4 * pairs),
        name="attention_forward",
    )(first, query, key, value)


def attention_backward_body(first, q_ref, k_ref, v_ref, grad_ref, context_ref, lse_ref, cosine, sine, *refs):
    dq_ref, dk_ref, dv_ref, dk_sum, dv_sum = refs[-5:]
    blocks = q_ref.shape[0] // QUERY_BLOCK
    scaled = q_ref[...].astype(F32) * HEAD_DIM**-0.5
    q_turned = scaled.T.astype(BF16)
    q_plain = scaled.astype(BF16)
    k_turned = k_ref[...].T
    grad = grad_ref[...]
    grad_turned = grad.T
    inner = (grad.astype(F32) * context_ref[...].astype(F32)).T
    square = (QUERY_BLOCK, QUERY_BLOCK)
    causal = lax.broadcasted_iota(jnp.int32, square, 0) <= lax.broadcasted_iota(jnp.int32, square, 1)
    low_lanes = lax.broadcasted_iota(jnp.int32, (QUERY_BLOCK, LANES), 1) < HEAD_DIM
    for i in reversed(range(blocks)):
        now = slice(i * QUERY_BLOCK, (i + 1) * QUERY_BLOCK)
        seen = slice(0, (i + 1) * QUERY_BLOCK)
        grads = []
        for h in range(2):
            head = slice(h * HEAD_DIM, (h + 1) * HEAD_DIM)
            own_lanes = low_lanes if h == 0 else jnp.logical_not(low_lanes)
            q_rows = jnp.where(own_lanes, q_plain[now, :], 0)
            g_rows = jnp.where(own_lanes, grad[now, :], 0)
            delta = jnp.sum(inner[head, now], axis=0, keepdims=True)
            lse = lse_ref[0, h : h + 1, now]
            scores = dot_nn(k_ref[seen, :], own_half(q_turned[head, now], h))
            grad_probs = dot_nn(v_ref[seen, :], own_half(grad_turned[head, now], h))
            probs, grad_scores = [], []
            for b in range(i + 1):
                there = slice(b * QUERY_BLOCK, (b + 1) * QUERY_BLOCK)
                part = scores[there]
                base = lse if b == i else lse + jnp.where(first[i] <= b, 0.0, -NEGATIVE)
                if b == i:
                    part = jnp.where(causal, part, NEGATIVE)
                part = jnp.exp2(part * LOG2E - base)
                probs.append(part.astype(BF16))
                grad_scores.append((part * (grad_probs[there] - delta)).astype(BF16))
            probs, grad_scores = jnp.concatenate(probs, axis=0), jnp.concatenate(grad_scores, axis=0)
            dv, dk = dot_nn(probs, g_rows), dot_nn(grad_scores, q_rows)
            if i == blocks - 1 and h == 0:
                dv_sum[...] = dv
                dk_sum[...] = dk
            else:
                dv_sum[seen, :] += dv
                dk_sum[seen, :] += dk
            grads.append(dot_nn(k_turned[head, seen], grad_scores) * HEAD_DIM**-0.5)
        dq = jnp.concatenate(grads, axis=0).T
        dq_ref[now, :] = (dq * cosine[now, :] - swap_halves(dq) * sine[now, :]).astype(BF16)
    dk = dk_sum[...]
    dk_ref[...] = (dk * cosine[...] - swap_halves(dk) * sine[...]).astype(BF16)
    dv_ref[...] = dv_sum[...].astype(BF16)


def attention_backward(first, query, key, value, grad, context, lse, cosine, sine, begin, pairs, into):
    tokens, width = query.shape
    spec = pl.BlockSpec((tokens, LANES), lambda j, f: (0, j + begin))
    table = pl.BlockSpec((tokens, LANES), lambda j, f: (0, 0))
    anywhere = pl.BlockSpec(memory_space=pl.ANY)
    return pl.pallas_call(
        attention_backward_body,
        grid_spec=pltpu.PrefetchScalarGridSpec(
            num_scalar_prefetch=1,
            grid=(pairs,),
            in_specs=[spec] * 5
            + [pl.BlockSpec((1, 8, tokens), lambda j, f: (j + begin, 0, 0)), table, table]
            + [anywhere] * len(into),
            out_specs=[spec] * 3,
            scratch_shapes=[pltpu.VMEM((tokens, LANES), F32)] * 2,
        ),
        out_shape=[jax.ShapeDtypeStruct((tokens, width), BF16)] * 3,
        input_output_aliases={9 + k: k for k in range(len(into))},
        cost_estimate=costs(6 * pairs),
        name="attention_backward",
    )(first, query, key, value, grad, context, lse, cosine, sine, *into)


def middle_tile(
    contexts, x, cotangent, w_output, w_gate, w_up, w_down, gains, ready,
    layer_out, hidden_in_turned, branch_two_turned, context_turned, hidden, grad_gate, grad_up, grad_first, branch_one, grad_context, gain_grads,
    slope, act,
):
    width = x.shape[1]
    span = w_gate.shape[1]
    chunk = 512
    ready(0)
    gain_one = gains[0:1, :]
    gain_two = gains[1:2, :]
    context_now = jnp.concatenate([part[...] for part in contexts], axis=1)
    first_sum = x[...].astype(F32) + dot_nn(context_now, w_output[...])
    scale_one = lax.rsqrt(jnp.mean(first_sum * first_sum, axis=1, keepdims=True) + EPSILON)
    normed_one = first_sum * scale_one
    normed = normed_one * gain_one
    hidden_in = normed.astype(BF16)
    second_sum = normed
    ready(1)
    for start in range(0, span, chunk):
        cols = slice(start, start + chunk)
        gate_act = dot_nn(hidden_in, w_gate[:, cols])
        up_act = dot_nn(hidden_in, w_up[:, cols])
        sigmoid = jax.nn.sigmoid(gate_act)
        silu = gate_act * sigmoid
        act[:, cols] = silu
        slope[:, cols] = up_act * (sigmoid + silu * (1.0 - sigmoid))
        hidden_now = (silu * up_act).astype(BF16)
        hidden[:, cols] = hidden_now
        if start == 0:
            ready(2)
        second_sum = second_sum + dot_nt(hidden_now, w_down[:, cols])
    scale_two = lax.rsqrt(jnp.mean(second_sum * second_sum, axis=1, keepdims=True) + EPSILON)
    normed_two = second_sum * scale_two
    layer_out[...] = (normed_two * gain_two).astype(BF16)
    grad_out = cotangent[...].astype(F32)
    two_term = jnp.sum(grad_out * normed_two, axis=0, keepdims=True)
    scaled = grad_out * gain_two
    grad_second = scale_two * (scaled - normed_two * jnp.mean(scaled * normed_two, axis=1, keepdims=True))
    branch_two = grad_second.astype(BF16)
    grad_normed = grad_second
    for start in range(0, span, chunk):
        cols = slice(start, start + chunk)
        grad_hidden = dot_nn(branch_two, w_down[:, cols])
        gate_now = (grad_hidden * slope[:, cols]).astype(BF16)
        up_now = (grad_hidden * act[:, cols]).astype(BF16)
        grad_gate[:, cols] = gate_now
        grad_up[:, cols] = up_now
        grad_normed = grad_normed + dot_nt(gate_now, w_gate[:, cols]) + dot_nt(up_now, w_up[:, cols])
    one_term = jnp.sum(grad_normed * normed_one, axis=0, keepdims=True)
    scaled = grad_normed * gain_one
    first_grad = scale_one * (scaled - normed_one * jnp.mean(scaled * normed_one, axis=1, keepdims=True))
    grad_first[...] = first_grad
    one_now = first_grad.astype(BF16)
    branch_one[...] = one_now
    grad_context[...] = dot_nt(one_now, w_output[...]).astype(BF16)
    hidden_in_turned[...] = hidden_in.T
    branch_two_turned[...] = branch_two.T
    context_turned[...] = context_now.T
    terms = jnp.concatenate([one_term, two_term, jnp.zeros((6, width), F32)], axis=0)

    @pl.when(pl.program_id(0) == 0)
    def _():
        gain_grads[...] = terms

    @pl.when(pl.program_id(0) > 0)
    def _():
        gain_grads[...] += terms


def middle_specs(tokens, width, span, rows):
    tile = pl.BlockSpec((rows, width), lambda i: (i, 0))
    wide = pl.BlockSpec((rows, span), lambda i: (i, 0))
    turned = pl.BlockSpec((width, rows), lambda i: (0, i))
    eight = pl.BlockSpec((8, width), lambda i: (0, 0))
    flat = jax.ShapeDtypeStruct((tokens, width), BF16)
    flat_turned = jax.ShapeDtypeStruct((width, tokens), BF16)
    broad = jax.ShapeDtypeStruct((tokens, span), BF16)
    return (
        [tile, turned, turned, turned, wide, wide, wide, tile, tile, tile, eight],
        [
            flat, flat_turned, flat_turned, flat_turned, broad, broad, broad,
            jax.ShapeDtypeStruct((tokens, width), F32), flat, flat, jax.ShapeDtypeStruct((8, width), F32),
        ],
    )


def middle_plain_body(context, x, cotangent, w_output, w_gate, w_up, w_down, gains, *rest):
    middle_tile((context,), x, cotangent, w_output, w_gate, w_up, w_down, gains, lambda k: None, *rest)


def middle_plain(context, x, cotangent, w_output, w_gate, w_up, w_down, gains):
    tokens, width = x.shape
    span = w_gate.shape[1]
    rows = 256
    tile = pl.BlockSpec((rows, width), lambda i: (i, 0))
    square = pl.BlockSpec((width, width), lambda i: (0, 0), pipeline_mode=pl.Buffered(1))
    whole = pl.BlockSpec((width, span), lambda i: (0, 0), pipeline_mode=pl.Buffered(1))
    eight = pl.BlockSpec((8, width), lambda i: (0, 0))
    out_specs, out_shape = middle_specs(tokens, width, span, rows)
    return pl.pallas_call(
        middle_plain_body,
        grid=(tokens // rows,),
        in_specs=[tile, tile, tile, square, whole, whole, whole, eight],
        out_specs=out_specs,
        out_shape=out_shape,
        scratch_shapes=[pltpu.VMEM((rows, span), F32)] * 2,
        name="feed_forward_and_back_plain",
    )(context, x, cotangent, w_output, w_gate, w_up, w_down, gains)


def middle_body(grid, count, place, *refs):
    pieces, refs = refs[:count], refs[count:]
    context, x, cotangent = refs[:3]
    outs = refs[3:14]
    slope, act, w_output, w_gate, w_up, w_down, gains, held, sems = refs[14:]
    here = pl.program_id(0) == 0

    @pl.when(here)
    def _():
        start_feed_copies(grid, place, pieces, w_gate, w_up, w_down, held, sems)

    def ready(k):
        @pl.when(here)
        def _():
            for n, target in (((0, held),), ((1, w_gate), (2, w_up)), ((3, w_down),))[k]:
                pltpu.make_async_copy(target, target, sems.at[n]).wait()
            if k == 0:
                assemble_output(grid, place, held, w_output, gains)

    middle_tile((context,), x, cotangent, w_output, w_gate, w_up, w_down, gains, ready, *outs, slope, act)


def middle(pieces, place, grid, context, x, cotangent):
    tokens, width = x.shape
    _, height, lanes = pieces[0].shape
    span = lanes * grid[1]
    rows = 256
    tile = pl.BlockSpec((rows, width), lambda i: (i, 0))
    anywhere = pl.BlockSpec(memory_space=pl.ANY)
    out_specs, out_shape = middle_specs(tokens, width, span, rows)
    return pl.pallas_call(
        lambda *refs: middle_body(grid, len(pieces), *refs),
        grid=(tokens // rows,),
        in_specs=[pl.BlockSpec(memory_space=pltpu.SMEM)] + [anywhere] * len(pieces) + [tile] * 3,
        out_specs=out_specs,
        out_shape=out_shape,
        scratch_shapes=[pltpu.VMEM((rows, span), F32)] * 2
        + [pltpu.VMEM((width, width), BF16)]
        + [pltpu.VMEM((width, span), BF16)] * 3
        + [
            pltpu.VMEM((8, width), F32),
            pltpu.VMEM((2, grid[0] * grid[1], height // 7, lanes), BF16),
            pltpu.SemaphoreType.DMA((4,)),
        ],
        cost_estimate=costs(40),
        name="feed_forward_and_back",
    )(place, *pieces, context, x, cotangent)


def part_of(index, place_index, core, count):
    far = index ^ place_index
    return jnp.where(core == 0, far, reversed_bits(far, bit_count(count)))


def store_split(own, low, high, where, grid, core_here, row, col, rows, lanes, halves):
    here = core_here == 0
    at = part_of(row, where[0], core_here, grid[0]), part_of(col, where[1], core_here, grid[1])
    own[at[0], at[1], rows, lanes] = jnp.where(here, halves[0], halves[1])
    at = part_of(row, where[0], 1 - core_here, grid[0]), part_of(col, where[1], 1 - core_here, grid[1])
    value = jnp.where(here, halves[1], halves[0])
    edge = grid[0] // 2

    @pl.when(at[0] < edge)
    def _():
        low[at[0], at[1], rows, lanes] = value

    @pl.when(at[0] >= edge)
    def _():
        high[at[0] - edge, at[1], rows, lanes] = value


def rest_tile(first, second, odd):
    low = split_rows(first.shape)
    rolled = pltpu.roll(second, 64, 1)
    return jnp.where(low, rolled, first) if odd else jnp.where(low, first, rolled)


def feed_grads_body(grid, count, place, left, *refs):
    rights, (own, other) = refs[:count], refs[-2:]
    grid_rows, grid_cols = grid
    half = left.shape[0] // grid_rows // 2
    here = place[2] == 0
    for k, right in enumerate(rights):
        product = dot_nn(left[...], right[...]).astype(BF16)
        rows = slice(k * half, (k + 1) * half)
        for i in range(grid_rows):
            first, second = (product[(2 * i + c) * half : (2 * i + c + 1) * half] for c in range(2))
            mine, theirs = part_of(i, place[0], place[2], grid_rows), part_of(i, place[0], 1 - place[2], grid_rows)
            own[mine, 0, rows, :] = jnp.where(here, first, second)
            other[theirs, 0, rows, :] = jnp.where(here, second, first)


def feed_grads(place, grid, left, rights):
    width, tokens = left.shape
    grid_rows, grid_cols = grid
    span = rights[0].shape[1] // grid_cols
    half = width // grid_rows // 2
    count = len(rights)

    def out_index(flip):
        return lambda i, s: (0, part_of(i, s[1], s[2] ^ flip, grid_cols), 0, 0)

    shape = (grid_rows, grid_cols, half * count, span)
    return pl.pallas_call(
        lambda *refs: feed_grads_body(grid, count, *refs),
        grid_spec=pltpu.PrefetchScalarGridSpec(
            num_scalar_prefetch=1,
            grid=(grid_cols,),
            in_specs=[pl.BlockSpec((width, tokens), lambda i, s: (0, 0), pipeline_mode=pl.Buffered(1))]
            + [pl.BlockSpec((tokens, span), lambda i, s: (0, i))] * count,
            out_specs=[pl.BlockSpec((grid_rows, 1, half * count, span), out_index(f)) for f in range(2)],
        ),
        out_shape=[jax.ShapeDtypeStruct(shape, BF16)] * 2,
        cost_estimate=costs(7 * count),
        name="feed_forward_weight_grad",
    )(place, left, *rights)


def down_grads_body(grid, place, branch_two_turned, hidden, context_turned, branch_one, gain_grads, own, other):
    grid_rows, grid_cols = grid
    width = branch_two_turned.shape[0]
    half = width // grid_cols // 2
    quarter = half // 2
    here = place[2] == 0
    row = pl.program_id(0)
    down = dot_nn(branch_two_turned[...], hidden[...]).astype(BF16)
    output = dot_nn(context_turned[...], branch_one[...])
    share = width // (grid_rows * grid_cols)
    lane = lax.broadcasted_iota(jnp.int32, (width, LANES), 0)
    gather = (lax.rem(lane, share) == lax.broadcasted_iota(jnp.int32, (width, LANES), 1)).astype(BF16)
    block_of = lax.div(lax.broadcasted_iota(jnp.int32, (8, width), 1), share)
    low = slice(half, half + quarter)

    def store(mine, theirs, rows, lanes, halves):
        own[0, mine, rows, lanes] = jnp.where(here, halves[0], halves[1])
        other[0, theirs, rows, lanes] = jnp.where(here, halves[1], halves[0])

    for c in range(grid_cols):
        at = part_of(c, place[1], place[2], grid_cols), part_of(c, place[1], 1 - place[2], grid_cols)
        store(*at, slice(0, half), slice(0, down.shape[1]), [down[(2 * c + k) * half : (2 * c + k + 1) * half] for k in range(2)])
        tile = 384 * (c // 2)
        odd = c % 2
        body = slice(tile + 256 * odd, tile + 256 * odd + 128)
        mid = slice(tile + 128, tile + 256)
        tops, lows = ([slice(k * half + n * quarter, k * half + (n + 1) * quarter) for k in range(2)] for n in range(2))
        store(*at, low, slice(0, 128), [output[t, body].astype(BF16) for t in tops])
        store(*at, low, slice(128, 256), [output[t, body].astype(BF16) for t in lows])
        store(*at, low, slice(256, 384), [rest_tile(output[t, mid], output[l, mid], odd).astype(BF16) for t, l in zip(tops, lows)])
        picked = jnp.where(block_of == row * grid_cols + c, gain_grads[...], 0.0).astype(BF16)
        gain = dot_nn(picked, gather)
        gain = jnp.concatenate([gain, jnp.zeros((quarter - 8, LANES), F32)], axis=0).astype(BF16)
        store(*at, low, slice(384, 512), [gain, gain])


def down_grads(place, grid, branch_two_turned, hidden, context_turned, branch_one, gain_grads):
    width, tokens = branch_two_turned.shape
    grid_rows, grid_cols = grid
    span = hidden.shape[1] // grid_rows
    half = width // grid_cols // 2
    height = half + half // 2

    def out_index(flip):
        return lambda i, s: (part_of(i, s[0], s[2] ^ flip, grid_rows), 0, 0, 0)

    once = dict(pipeline_mode=pl.Buffered(1))
    own, other = pl.pallas_call(
        lambda *refs: down_grads_body(grid, *refs),
        grid_spec=pltpu.PrefetchScalarGridSpec(
            num_scalar_prefetch=1,
            grid=(grid_rows,),
            in_specs=[
                pl.BlockSpec((width, tokens), lambda i, s: (0, 0), **once),
                pl.BlockSpec((tokens, span), lambda i, s: (0, i)),
                pl.BlockSpec((width // grid_rows, tokens), lambda i, s: (i, 0)),
                pl.BlockSpec((tokens, width), lambda i, s: (0, 0), **once),
                pl.BlockSpec((8, width), lambda i, s: (0, 0)),
            ],
            out_specs=[pl.BlockSpec((1, grid_cols, height, span), out_index(f)) for f in range(2)],
        ),
        out_shape=[jax.ShapeDtypeStruct((grid_rows, grid_cols, height, span), BF16)] * 2,
        cost_estimate=costs(10),
        name="down_weight_grad",
    )(place, branch_two_turned, hidden, context_turned, branch_one, gain_grads)
    return own, other


def attention_grads_body(grid, place, x_turned, grad_query, grad_key, grad_value, own, lower, upper):
    grid_rows, grid_cols = grid
    where = (place[0], place[1])
    half = x_turned.shape[0] // grid_rows // 2
    quarter = half // 2
    pair = pl.program_id(0)
    query, key, value = (dot_nn(x_turned[...], g[...]) for g in (grad_query, grad_key, grad_value))
    mid = slice(128, 256)
    for row in range(grid_rows):
        for odd in range(2):
            body = slice(256 * odd, 256 * odd + 128)
            pieces = []
            for core in range(2):
                start = row * 2 * half + core * half
                rows = slice(start, start + half)
                top, low = slice(start, start + quarter), slice(start + quarter, start + half)
                joined = (query[rows, body], key[rows, body], rest_tile(query[rows, mid], key[rows, mid], odd))
                last = (value[top, body], value[low, body], rest_tile(value[top, mid], value[low, mid], odd))
                pieces.append([p.astype(BF16) for p in joined + last])
            for k in range(3):
                lanes = slice(128 * k, 128 * (k + 1))
                at = (row, 2 * pair + odd)
                for n, rows in ((k, slice(0, half)), (3 + k, slice(half, half + quarter))):
                    store_split(own, lower, upper, where, grid, place[2], *at, rows, lanes, [p[n] for p in pieces])


def attention_grads(place, grid, x_turned, grads):
    width, tokens = x_turned.shape
    grid_rows, grid_cols = grid
    half = width // grid_rows // 2
    shape = (grid_rows, grid_cols, half + half // 2, 384)
    half_shape = (grid_rows // 2, *shape[1:])
    out, part = (pl.BlockSpec(v, lambda i, s: (0, 0, 0, 0), pipeline_mode=pl.Buffered(1)) for v in (shape, half_shape))
    return pl.pallas_call(
        lambda *refs: attention_grads_body(grid, *refs),
        grid_spec=pltpu.PrefetchScalarGridSpec(
            num_scalar_prefetch=1,
            grid=(width // 384,),
            in_specs=[pl.BlockSpec((width, tokens), lambda i, s: (0, 0), pipeline_mode=pl.Buffered(1))]
            + [pl.BlockSpec((tokens, 384), lambda i, s: (0, i))] * 3,
            out_specs=[out, part, part],
        ),
        out_shape=[jax.ShapeDtypeStruct(v, BF16) for v in (shape, half_shape, half_shape)],
        cost_estimate=costs(8),
        name="attention_weight_grads",
    )(place, x_turned, *grads)


def input_grad_body(grad_first, grad_query, grad_key, grad_value, w_query, w_key, w_value, out):
    total = grad_first[...]
    for grad, weight in ((grad_query, w_query), (grad_key, w_key), (grad_value, w_value)):
        total = total + dot_nt(grad[...], weight[...])
    out[...] = total.astype(BF16)


def input_gradient(grad_first, grads, w_query, w_key, w_value):
    tokens, width = grad_first.shape
    rows = 256
    tile = pl.BlockSpec((rows, width), lambda i: (i, 0))
    whole = pl.BlockSpec((width, width), lambda i: (0, 0), pipeline_mode=pl.Buffered(1))
    return pl.pallas_call(
        input_grad_body,
        grid=(tokens // rows,),
        in_specs=[tile] * 4 + [whole] * 3,
        out_specs=tile,
        out_shape=jax.ShapeDtypeStruct((tokens, width), BF16),
        cost_estimate=costs(8),
        name="input_gradient",
    )(grad_first, *grads, w_query, w_key, w_value)


def gather_plain(block):
    whole = lax.all_gather(block, "col", axis=1, tiled=True)
    return lax.all_gather(whole, "row", axis=0, tiled=True)


def scatter_plain(whole):
    part = lax.psum_scatter(whole.astype(BF16), "row", scatter_dimension=0, tiled=True)
    part = lax.psum_scatter(part, "col", scatter_dimension=1, tiled=True)
    return lax.psum(part, "dp").astype(F32)


def scatter_gain(whole):
    part = lax.psum_scatter(whole.astype(BF16), ("row", "col"), scatter_dimension=0, tiled=True)
    return lax.psum(part, "dp").astype(F32)


def on_device(
    inputs,
    segment_ids,
    query_weight,
    key_weight,
    value_weight,
    output_weight,
    gate_weight,
    up_weight,
    down_weight,
    first_gain,
    second_gain,
    cotangent,
):
    grid = (lax.axis_size("row"), lax.axis_size("col"))
    tokens, width = inputs.shape
    hidden_width = gate_weight.shape[1] * grid[1]
    core = lax.axis_index("dp")
    odd = (lax.axis_index("col") & 1) == 1
    place = place_scalars()
    packs = grid == (4, 4) and query_weight.shape[1] == 192 and gate_weight.shape[1] == 512

    def tables(segments):
        token_index = jnp.arange(tokens, dtype=jnp.int32)
        length = tokens // (segments[tokens - 1] + 1)
        starts = segments * length
        positions = (token_index - starts).astype(F32)
        frequencies = ROPE_BASE ** (-2.0 * jnp.arange(HEAD_DIM // 2, dtype=F32) / HEAD_DIM)
        phases = positions[:, None] * frequencies[None, :]
        cosine, sine = jnp.cos(phases), jnp.sin(phases)
        cosine = jnp.concatenate([cosine] * 4, axis=1)
        sine = jnp.concatenate([-sine, sine] * 2, axis=1)
        return cosine, sine, starts[::QUERY_BLOCK] // QUERY_BLOCK

    def backward(grad_context, context, lse, begin, pairs, into):
        return attention_backward(first, query, key, value, grad_context, context, lse, cosine, sine, begin, pairs, into)

    if not packs:
        cosine, sine, first = tables(segment_ids)
        x_turned = inputs.T
        w_query, w_key, w_value, w_output = (
            gather_plain(w) for w in (query_weight, key_weight, value_weight, output_weight)
        )
        w_gate, w_up, w_down = gather_plain(gate_weight), gather_plain(up_weight), gather_plain(down_weight).T
        gains = jnp.stack(
            [lax.all_gather(g, ("row", "col"), axis=0, tiled=True).astype(F32) for g in (first_gain, second_gain)]
        )
        gains = jnp.pad(gains, ((0, 6), (0, 0)))
        query, key, value = project(inputs, w_query, w_key, w_value, cosine, sine)
        context, lse = attention_forward(first, query, key, value, 0, width // LANES)
        (
            layer_out, hidden_in_turned, branch_two_turned, context_turned, hidden, grad_gate, grad_up, grad_first, branch_one, grad_context, gain_grads,
        ) = middle_plain(context, inputs, cotangent, w_output, w_gate, w_up, w_down, gains)
        grads = backward(grad_context, context, lse, 0, width // LANES, ())
        input_grad = input_gradient(grad_first, grads, w_query, w_key, w_value)
        query_out, key_out, value_out = (scatter_plain(dot_nn(x_turned, g)) for g in grads)
        output_out = scatter_plain(dot_nn(context_turned, branch_one))
        gate_out, up_out = (scatter_plain(dot_nn(hidden_in_turned, g)) for g in (grad_gate, grad_up))
        down_out = scatter_plain(dot_nn(branch_two_turned, hidden).T)
        gain_one_out, gain_two_out = scatter_gain(gain_grads[0]), scatter_gain(gain_grads[1])
        return (
            layer_out, input_grad, query_out, key_out, value_out, output_out, gate_out, up_out, down_out, gain_one_out, gain_two_out,
        )

    join = lambda *stacks: jnp.concatenate(stacks, axis=0)
    q0 = pack_attention(place, query_weight, key_weight, value_weight)[None]
    f0 = pack_feed(place, gate_weight, up_weight, down_weight.T, output_weight, first_gain, second_gain)[None]
    q1 = exchange(q0, grid, 0)
    f1 = exchange(f0, grid, 0)
    q1, f0, segments, x_in = tie(q1, f0, segment_ids, inputs)
    q01 = join(q0, q1)
    q2 = exchange(q01, grid, 1)
    cosine, sine, first = tables(segments)
    x_turned = x_in.T
    q2, f1, cosine, sine, x_turned, first = tie(q2, f1, cosine, sine, x_turned, first)
    q03 = join(q01, q2)
    f01 = join(f0, f1)
    q3, q4 = exchange(q03, grid, 2), exchange(q03, grid, 3)
    q03_other = other_core(q03)
    f2 = exchange(f01, grid, 1)
    q3, q4, q03_other = tie(q3, q4, q03_other)
    q5 = exchange(q3, grid, 3)
    q3_other, q4_other = other_core(q3), other_core(q4)
    q5, q3_other, q4_other, f2 = tie(q5, q3_other, q4_other, f2)
    q5_other = other_core(q5)
    f03 = join(f01, f2)
    f3, f4 = exchange(f03, grid, 2), exchange(f03, grid, 3)
    query, key, value, w_query, w_key, w_value = project_blocks(
        (q03, q3, q4, q5, q03_other, q3_other, q4_other, q5_other), place, grid, inputs, cosine, sine
    )
    f03_other = other_core(f03)
    context, lse = attention_forward(first, query, key, value, 0, width // LANES)
    f3, f4, f03_other, context = tie(f3, f4, f03_other, context)
    f5 = exchange(f3, grid, 3)
    f3_other, f4_other = other_core(f3), other_core(f4)
    f5, f3_other, f4_other = tie(f5, f3_other, f4_other)
    (
        layer_out, hidden_in_turned, branch_two_turned, context_turned, hidden, grad_gate, grad_up, grad_first, branch_one, grad_context, gain_grads,
    ) = middle((f03, f3, f4, f5, f03_other, f3_other, f4_other, other_core(f5)), place, grid, context, inputs, cotangent)

    pairs = width // LANES
    feed = Scatter(grid)
    own, other = feed_grads(place, grid, hidden_in_turned, (grad_gate, grad_up))
    other, branch_two_turned = tie(other, branch_two_turned)
    received = other_core(other)
    low_own, low_other = down_grads(place, grid, branch_two_turned, hidden, context_turned, branch_one, gain_grads)
    received, low_other = tie(received, low_other)
    feed.add(own, received)
    feed.add(low_own, other_core(low_other))
    came = feed.send(feed.sums([2, 0], [2, 4]), 3)
    grads = backward(grad_context, context, lse, 0, pairs // 2, ())
    grads = backward(grad_context, context, lse, pairs // 2, pairs // 2, grads)
    came, x_turned, grads = tie(came, x_turned, grads)
    feed.put(came)
    away, x_turned = tie(feed.sums([1, 0], [1, 4]), x_turned)
    came = feed.send(away, 2)
    heads = Scatter(grid)
    own, low, high = attention_grads(place, grid, x_turned, grads)
    heads.add(own)
    heads.put(other_core(low))
    heads.put(other_core(high), (2, 0))
    away, came = tie(heads.sums([2, 0], [2, 4]), came)
    came_heads = heads.send(away, 3)
    feed.put(came)
    away, grad_first = tie(feed.sums([0, 2], [1, 2]), grad_first)
    came = feed.send(away, 1)
    input_grad = input_gradient(grad_first, grads, w_query, w_key, w_value)
    came_heads, input_grad = tie(came_heads, input_grad)
    heads.put(came_heads)
    came_heads = heads.send(heads.sums([1, 0], [1, 4]), 2)
    feed.put(came)
    came_heads, away = tie(came_heads, feed.sums([0, 1], [1, 1]))
    came = feed.send(away, 0)
    heads.put(came_heads)
    came_heads = heads.send(heads.sums([0, 2], [1, 2]), 1)
    heads.put(came_heads)
    came_heads, came = tie(heads.send(heads.sums([0, 1], [1, 1]), 0), came)
    heads.put(came_heads)
    feed.put(came)
    mine = last_sums((feed, heads))
    query_out, key_out, value_out, output_out, gate_out, up_out, down_out, gain_one_out, gain_two_out = finish(
        place, mine, other_core(mine), [query_weight.shape] * 4 + [gate_weight.shape] * 3 + [first_gain.shape] * 2
    )
    return (
        layer_out, input_grad, query_out, key_out, value_out, output_out, gate_out, up_out, down_out.T, gain_one_out, gain_two_out,
    )


def solution(mesh):
    tokens = P(("dp", "row", "col"), None)
    block = P("row", "col")
    gain = P(("row", "col"))
    return jax.shard_map(
        on_device,
        mesh=mesh,
        in_specs=(tokens, P(("dp", "row", "col"))) + (block,) * 7 + (gain, gain, tokens),
        out_specs=(tokens, tokens) + (block,) * 7 + (gain, gain),
        check_vma=False,
    )
```

profile of v0, /device:TPU:0, one launch (start us, length us, event | category | flops | bytes accessed | tf_op | source)
XLA Modules:
  0.0 291.5 jit_solution(3370366232343034364)
XLA Ops:
  1.3 1.8 pack_attention.1
  3.0 3.0 %collective-permute-start = (bf16[1,144,384]{2,1,0:T(8,128)(2,1)}, bf16[1,144,384]{2,1,0:T(8,128)(2,1)S(1)}, u32[]{:S(2)}, u32[]{:S(2)}) collective-permute-start(bf16[1,144,384]{2,1,0:T(8,128)(2,1)} %bitcast.16), channel_id=1, source_target_pairs={{0,1},{1,0},{2,3},{3,2},{4,5},{5,4},{6,7},{7,6},{8,9},{9,8},{10,11... | collective-permute-start | bytes 331784 | tf_op jit(solution)/shard_map/ppermute | solution.py:61
  6.1 2.0 pack_feed.1
  8.1 2.0 collective-permute-done
  10.1 1.3 slice.45
  13.8 2.2 collective-permute-start.1
  16.0 1.7 copy.28
  17.7 1.9 fusion
  19.6 1.9 pad_maximum_fusion.1
  23.9 1.5 collective-permute-start.4
  25.5 1.5 collective-permute-start.3
  27.0 1.7 collective-permute-start.9
  28.7 7.9 %collective-permute-done.4.refs_3_ = bf16[4,144,384]{2,1,0:T(8,128)(2,1)S(1)} collective-permute-done((bf16[4,144,384]{2,1,0:T(8,128)(2,1)S(1)}, bf16[4,144,384]{2,1,0:T(8,128)(2,1)S(1)}, u32[]{:S(2)}, u32[]{:S(2)}) %collective-permute-start.4) | collective-permute-done | bytes 442400 | tf_op jit(solution)/shard_map/ppermute | solution.py:61
  37.2 1.5 collective-permute-start.6
  38.8 7.5 %collective-permute-done.9 = bf16[2,336,512]{2,1,0:T(8,128)(2,1)S(1)} collective-permute-done((bf16[2,336,512]{2,1,0:T(8,128)(2,1)S(1)}, bf16[2,336,512]{2,1,0:T(8,128)(2,1)S(1)}, u32[]{:S(2)}, u32[]{:S(2)}) %collective-permute-start.9) | collective-permute-done | bytes 688160 | tf_op jit(solution)/shard_map/ppermute | solution.py:61
  49.2 2.8 collective-permute-done.13.refs_8_
  51.9 11.0 %project_heads.1 = (bf16[1024,768]{1,0:T(8,128)(2,1)}, bf16[1024,768]{1,0:T(8,128)(2,1)}, bf16[1024,768]{1,0:T(8,128)(2,1)}, bf16[768,768]{1,0:T(8,128)(2,1)}, b...) custom-call(s32[3]{0:T(128)} %pad_add_fusion.place.refs_0_, bf16[4,144,384]{2,1,0:T(8,128)(2,1)} %copy-done.9, ...), custom_call_target="tpu_custom_call" | custom-call | flops 100000000 | bytes 100000 | tf_op jit(solution)/shard_map/project_heads/pallas_call | solution.py:490
  62.9 12.9 %attention_forward.1 = (bf16[1024,768]{1,0:T(8,128)(2,1)}, f32[6,8,1024]{2,1,0:T(8,128)}) custom-call(s32[4]{0:T(128)} %and_select_fusion.first, bf16[1024,768]{1,0:T(8,128)(2,1)} %get-tuple-element.113.q_ref, bf16[1024,768]{1,0:T(8,128)(2,1)} %get-tuple-element.114.k_ref, bf16[1024,768]{1,0:T(8,128)(2,1)} %get-tuple-element.115.v_ref), custom_call_target="tpu_custom_call" | custom-call | flops 240000000 | bytes 240000 | tf_op jit(solution)/shard_map/attention_forward/pallas_call | solution.py:570
  75.9 5.1 %collective-permute-done.11.refs_3_ = bf16[4,336,512]{2,1,0:T(8,128)(2,1)} collective-permute-done((bf16[4,336,512]{2,1,0:T(8,128)(2,1)S(1)}, bf16[4,336,512]{2,1,0:T(8,128)(2,1)}, u32[]{:S(2)}, u32[]{:S(2)}) %collective-permute-start.11) | collective-permute-done | bytes 1376288 | tf_op jit(solution)/shard_map/ppermute | solution.py:61
  82.0 4.3 %collective-permute-done.16.refs_7_ = bf16[4,336,512]{2,1,0:T(8,128)(2,1)S(1)} collective-permute-done((bf16[4,336,512]{2,1,0:T(8,128)(2,1)}, bf16[4,336,512]{2,1,0:T(8,128)(2,1)S(1)}, u32[]{:S(2)}, u32[]{:S(2)}) %collective-permute-start.16) | collective-permute-done | bytes 1376288 | tf_op jit(solution)/shard_map/ppermute | solution.py:57
  86.4 13.6 %collective-permute-done.14.refs_4_ = bf16[4,336,512]{2,1,0:T(8,128)(2,1)S(1)} collective-permute-done((bf16[4,336,512]{2,1,0:T(8,128)(2,1)}, bf16[4,336,512]{2,1,0:T(8,128)(2,1)S(1)}, u32[]{:S(2)}, u32[]{:S(2)}) %collective-permute-start.14) | collective-permute-done | bytes 1376288 | tf_op jit(solution)/shard_map/ppermute | solution.py:61
  101.2 3.3 %collective-permute-done.17.refs_8_ = bf16[4,336,512]{2,1,0:T(8,128)(2,1)} collective-permute-done((bf16[4,336,512]{2,1,0:T(8,128)(2,1)S(1)}, bf16[4,336,512]{2,1,0:T(8,128)(2,1)}, u32[]{:S(2)}, u32[]{:S(2)}) %collective-permute-start.17) | collective-permute-done | bytes 1376288 | tf_op jit(solution)/shard_map/ppermute | solution.py:57
  104.4 41.2 %feed_forward_and_back.1 = (bf16[1024,768]{1,0:T(8,128)(2,1)}, bf16[768,1024]{1,0:T(8,128)(2,1)}, bf16[768,1024]{1,0:T(8,128)(2,1)}, bf16[768,1024]{1,0:T(8,128)...) custom-call(s32[3]{0:T(128)} %pad_add_fusion.place.refs_0_, ...), custom_call_target="tpu_custom_call" | custom-call | flops 400000000 | bytes 400000 | tf_op jit(solution)/shard_map/feed_forward_and_back/pallas_call | solution.py:803
  145.6 11.6 %feed_forward_weight_grad.1 = (bf16[4,4,192,512]{3,2,1,0:T(8,128)(2,1)}, bf16[4,4,192,512]{3,2,1,0:T(8,128)(2,1)}) custom-call(s32[3]{0:T(128)} %pad_add_fusion.place.refs_0_, bf16[768,1024]{1,0:T(8,128)(2,1)} %get-tuple-element.125.refs_1_, bf16[1024,2048]{1,0:T(8,128)(2,1)} %get-tuple-element.126.refs_2_, bf16[1024,2048]{1,0:T(8,128)(2,1)} %get-tuple-element.127.refs_3_), custom_call_target="tpu_custom_call" | custom-call | flops 140000000 | bytes 140000 | tf_op jit(solution)/shard_map/feed_forward_weight_grad/pallas_call | solution.py:876
  157.3 10.5 %down_weight_grad.1 = (bf16[4,4,144,512]{3,2,1,0:T(8,128)(2,1)}, bf16[4,4,144,512]{3,2,1,0:T(8,128)(2,1)}) custom-call(s32[3]{0:T(128)} %pad_add_fusion.place.refs_0_, bf16[768,1024]{1,0:T(8,128)(2,1)} %get-tuple-element.132.refs_1_, bf16[1024,2048]{1,0:T(8,128)(2,1)} %get-tuple-element.133.refs_2_, bf16[768,1024]{1,0:T(8,128)(2,1)} %get-tuple-element.134.refs_3_, ...), custom_call_target="tpu_custom_call" | custom-call | flops 100000000 | bytes 100000 | tf_op jit(solution)/shard_map/down_weight_grad/pallas_call | solution.py:938
  168.3 4.5 %collective-permute-done.19.refs_3_ = bf16[4,4,144,512]{3,2,1,0:T(8,128)(2,1)} collective-permute-done((bf16[4,4,144,512]{3,2,1,0:T(8,128)(2,1)}, bf16[4,4,144,512]{3,2,1,0:T(8,128)(2,1)}, u32[]{:S(2)}, u32[]{:S(2)}) %collective-permute-start.19) | collective-permute-done | bytes 2359328 | tf_op jit(solution)/shard_map/ppermute | solution.py:57
  172.8 4.0 %sum_blocks.4 = bf16[2,4,336,512]{3,2,1,0:T(8,128)(2,1)} custom-call(bf16[4,4,192,512]{3,2,1,0:T(8,128)(2,1)} %get-tuple-element.128.refs_0_, bf16[4,4,192,512]{3,2,1,0:T(8,128)(2,1)} %copy-done, bf16[4,4,144,512]{3,2,1,0:T(8,128)(2,1)} %get-tuple-element.139.refs_2_, bf16[4,4,144,512]{3,2,1,0:T(8,128)(2,1)} %collective-permute-done.19.refs_3_), custom_call_target="tpu_custom_call" | custom-call | flops 20000000 | bytes 20000 | tf_op jit(solution)/shard_map/sum_blocks/pallas_call | solution.py:128
  177.2 14.9 %attention_backward.2 = (bf16[1024,768]{1,0:T(8,128)(2,1)}, bf16[1024,768]{1,0:T(8,128)(2,1)}, bf16[1024,768]{1,0:T(8,128)(2,1)}) custom-call(s32[4]{0:T(128)} %and_select_fusion.first, bf16[1024,768]{1,0:T(8,128)(2,1)} %get-tuple-element.113.q_ref, bf16[1024,768]{1,0:T(8,128)(2,1)} %get-tuple-element.114.k_ref, bf16[1024,768]{1,0:T(8,128)(2,1)} %get-tuple-element.115.v_ref, ...), custom_call_target="tpu_custom_call" | custom-call | flops 180000000 | bytes 180000 | tf_op jit(solution)/shard_map/attention_backward/pallas_call | solution.py:644
  192.2 14.7 %attention_backward.3 = (bf16[1024,768]{1,0:T(8,128)(2,1)}, bf16[1024,768]{1,0:T(8,128)(2,1)}, bf16[1024,768]{1,0:T(8,128)(2,1)}) custom-call(s32[4]{0:T(128)} %and_select_fusion.first, bf16[1024,768]{1,0:T(8,128)(2,1)} %get-tuple-element.113.q_ref, ...), custom_call_target="tpu_custom_call", output_to_operand_aliasing={{0}: (9, {}), {1}: (10, {}), {2}: (11, {})} | custom-call | flops 180000000 | bytes 180000 | tf_op jit(solution)/shard_map/attention_backward/pallas_call | solution.py:644
  206.9 3.1 %collective-permute-done.20.refs_4_ = bf16[2,4,336,512]{3,2,1,0:T(8,128)(2,1)S(1)} collective-permute-done((bf16[2,4,336,512]{3,2,1,0:T(8,128)(2,1)}, bf16[2,4,336,512]{3,2,1,0:T(8,128)(2,1)S(1)}, u32[]{:S(2)}, u32[]{:S(2)}) %collective-permute-start.20) | collective-permute-done | bytes 2752544 | tf_op jit(solution)/shard_map/ppermute | solution.py:61
  210.0 1.6 copy-done.1
  211.6 3.2 %sum_blocks.5 = bf16[1,4,336,512]{3,2,1,0:T(8,128)(2,1)} custom-call(bf16[4,4,192,512]{3,2,1,0:T(8,128)(2,1)} %get-tuple-element.128.refs_0_, bf16[4,4,192,512]{3,2,1,0:T(8,128)(2,1)} %copy-done, bf16[4,4,144,512]{3,2,1,0:T(8,128)(2,1)} %get-tuple-element.139.refs_2_, bf16[4,4,144,512]{3,2,1,0:T(8,128)(2,1)} %collective-permute-done.19.refs_3_, ...), custom_call_target="tpu_custom_call" | custom-call | flops 20000000 | bytes 20000 | tf_op jit(solution)/shard_map/sum_blocks/pallas_call | solution.py:128
  215.1 12.7 %attention_weight_grads.1 = (bf16[4,4,144,384]{3,2,1,0:T(8,128)(2,1)}, bf16[2,4,144,384]{3,2,1,0:T(8,128)(2,1)}, bf16[2,4,144,384]{3,2,1,0:T(8,128)(2,1)}) custom-call(s32[3]{0:T(128)} %pad_add_fusion.place.refs_0_, bf16[768,1024]{1,0:T(8,128)(2,1)} %bitcast.12, bf16[1024,768]{1,0:T(8,128)(2,1)} %get-tuple-element.153.refs_2_.grad_query, ...), custom_call_target="tpu_custom_call" | custom-call | flops 80000000 | bytes 80000 | tf_op jit(solution)/shard_map/attention_weight_grads/pallas_call | solution.py:992
  227.8 2.6 collective-permute-done.21
  230.5 2.2 slice_add_fusion
  234.5 2.7 sum_blocks.6
  237.2 1.3 collective-permute-start.24
  238.5 8.6 %input_gradient.1 = bf16[1024,768]{1,0:T(8,128)(2,1)} custom-call(f32[1024,768]{1,0:T(8,128)} %get-tuple-element.162.grad_first, bf16[1024,768]{1,0:T(8,128)(2,1)} %get-tuple-element.153.refs_2_.grad_query, bf16[1024,768]{1,0:T(8,128)(2,1)} %get-tuple-element.154.refs_3_.grad_key, bf16[1024,768]{1,0:T(8,128)(2,1)} %get-tuple-element.155.refs_4_.grad_value, ...), custom_call_target="tpu_custom_call" | custom-call | flops 80000000 | bytes 80000 | tf_op jit(solution)/shard_map/input_gradient/pallas_call | solution.py:1019
  247.2 1.5 add_convert_fusion
  249.8 6.8 %collective-permute-done.24.refs_6_ = bf16[1,2,336,512]{3,2,1,0:T(8,128)(2,1)S(1)} collective-permute-done((bf16[1,2,336,512]{3,2,1,0:T(8,128)(2,1)}, bf16[1,2,336,512]{3,2,1,0:T(8,128)(2,1)S(1)}, u32[]{:S(2)}, u32[]{:S(2)}) %collective-permute-start.24) | collective-permute-done | bytes 688160 | tf_op jit(solution)/shard_map/ppermute | solution.py:61
  257.5 2.4 sum_blocks.7
  259.9 1.2 add_convert_fusion.1
  261.6 2.6 collective-permute-start.29
  264.2 11.7 %collective-permute-done.27.refs_12_ = bf16[1,2,144,384]{3,2,1,0:T(8,128)(2,1)S(1)} collective-permute-done((bf16[1,2,144,384]{3,2,1,0:T(8,128)(2,1)S(1)}, bf16[1,2,144,384]{3,2,1,0:T(8,128)(2,1)S(1)}, u32[]{:S(2)}, u32[]{:S(2)}) %collective-permute-start.27) | collective-permute-done | bytes 221216 | tf_op jit(solution)/shard_map/ppermute | solution.py:61
  277.1 4.7 %collective-permute-done.28.refs_13_ = bf16[1,1,144,384]{3,2,1,0:T(8,128)(2,1)S(1)} collective-permute-done((bf16[1,1,144,384]{3,2,1,0:T(8,128)(2,1)S(1)}, bf16[1,1,144,384]{3,2,1,0:T(8,128)(2,1)S(1)}, u32[]{:S(2)}, u32[]{:S(2)}) %collective-permute-start.28) | collective-permute-done | bytes 110624 | tf_op jit(solution)/shard_map/ppermute | solution.py:61
  283.2 2.9 last_sums.1.mine
  286.0 2.1 collective-permute-done.30.theirs
  288.9 2.6 finish.1
  (100 shorter events, 19.6 us)
Async XLA Ops:
  0.6 15.4 %copy-start.2 = (bf16[1024,768]{1,0:T(8,128)(2,1)S(1)}, bf16[1024,768]{1,0:T(8,128)(2,1)}, u32[]{:S(2)}) copy-start(bf16[1024,768]{1,0:T(8,128)(2,1)} %refs_10_.1) | copy-start | bytes 4718596
  3.0 7.1 %collective-permute-start = (bf16[1,144,384]{2,1,0:T(8,128)(2,1)}, bf16[1,144,384]{2,1,0:T(8,128)(2,1)S(1)}, u32[]{:S(2)}, u32[]{:S(2)}) collective-permute-start(bf16[1,144,384]{2,1,0:T(8,128)(2,1)} %bitcast.16), channel_id=1, source_target_pairs={{0,1},{1,0},{2,3},{3,2},{4,5},{5,4},{6,7},{7,6},{8,9},{9,8},{10,11... | collective-permute-start | bytes 331784 | tf_op jit(solution)/shard_map/ppermute | solution.py:61
  8.1 15.0 %collective-permute-start.2 = (bf16[1,336,512]{2,1,0:T(8,128)(2,1)}, bf16[1,336,512]{2,1,0:T(8,128)(2,1)S(1)}, u32[]{:S(2)}, u32[]{:S(2)}) collective-permute-start(bf16[1,336,512]{2,1,0:T(8,128)(2,1)} %bitcast.13), channel_id=1, source_target_pairs={{0,1},{1,0},{2,3},{3,2},{4,5},{5,4},{6,7},{7,6},{8,9},{9,8},{10,11... | collective-permute-start | bytes 1032200 | tf_op jit(solution)/shard_map/ppermute | solution.py:61
  13.8 9.3 %collective-permute-start.1 = (bf16[2,144,384]{2,1,0:T(8,128)(2,1)S(1)}, bf16[2,144,384]{2,1,0:T(8,128)(2,1)S(1)}, u32[]{:S(2)}, u32[]{:S(2)}) collective-permute-start(bf16[2,144,384]{2,1,0:T(8,128)(2,1)S(1)} %pad_maximum_fusion.4), channel_id=1, source_target_pairs={{0,2},{1,3},{2,0},{3,1},{4,6},{5,7},{6,4},{7,5},{8,10},{9,11},{10,... | collective-permute-start | bytes 663560 | tf_op jit(solution)/shard_map/ppermute | solution.py:61
  19.6 3.5 %copy-start.14 = (bf16[144,384]{1,0:T(8,128)(2,1)S(1)}, bf16[144,384]{1,0:T(8,128)(2,1)}, u32[]{:S(2)}) copy-start(bf16[144,384]{1,0:T(8,128)(2,1)} %pack_attention.1) | copy-start | bytes 331780
  19.6 7.4 %copy-start.6 = (bf16[336,512]{1,0:T(8,128)(2,1)S(1)}, bf16[336,512]{1,0:T(8,128)(2,1)}, u32[]{:S(2)}) copy-start(bf16[336,512]{1,0:T(8,128)(2,1)} %pack_feed.1) | copy-start | bytes 1032196
  23.2 24.8 %copy-start.9 = (bf16[4,144,384]{2,1,0:T(8,128)(2,1)}, bf16[4,144,384]{2,1,0:T(8,128)(2,1)S(1)}, u32[]{:S(2)}) copy-start(bf16[4,144,384]{2,1,0:T(8,128)(2,1)S(1)} %pad_maximum_fusion.3.refs_1_) | copy-start | bytes 1327108
  23.2 5.5 %collective-permute-start.5 = (bf16[4,144,384]{2,1,0:T(8,128)(2,1)S(1)}, bf16[4,144,384]{2,1,0:T(8,128)(2,1)S(1)}, u32[]{:S(2)}, u32[]{:S(2)}) collective-permute-start(bf16[4,144,384]{2,1,0:T(8,128)(2,1)S(1)} %pad_maximum_fusion.3.refs_1_), channel_id=1, source_target_pairs={{0,16},{16,0},{1,17},{17,1},{2,18},{18,2},{3,19},{19,3},{4,20},{20... | collective-permute-start | bytes 1327112 | tf_op jit(solution)/shard_map/ppermute | solution.py:57
  23.9 12.7 %collective-permute-start.4 = (bf16[4,144,384]{2,1,0:T(8,128)(2,1)S(1)}, bf16[4,144,384]{2,1,0:T(8,128)(2,1)S(1)}, u32[]{:S(2)}, u32[]{:S(2)}) collective-permute-start(bf16[4,144,384]{2,1,0:T(8,128)(2,1)S(1)} %pad_maximum_fusion.3.refs_1_), channel_id=1, source_target_pairs={{0,8},{1,9},{2,10},{3,11},{4,12},{5,13},{6,14},{7,15},{8,0},{9,1},... | collective-permute-start | bytes 1327112 | tf_op jit(solution)/shard_map/ppermute | solution.py:61
  25.5 11.2 %collective-permute-start.3 = (bf16[4,144,384]{2,1,0:T(8,128)(2,1)S(1)}, bf16[4,144,384]{2,1,0:T(8,128)(2,1)S(1)}, u32[]{:S(2)}, u32[]{:S(2)}) collective-permute-start(bf16[4,144,384]{2,1,0:T(8,128)(2,1)S(1)} %pad_maximum_fusion.3.refs_1_), channel_id=1, source_target_pairs={{0,4},{1,5},{2,6},{3,7},{4,0},{5,1},{6,2},{7,3},{8,12},{9,13},{10,... | collective-permute-start | bytes 1327112 | tf_op jit(solution)/shard_map/ppermute | solution.py:61
  27.0 19.3 %collective-permute-start.9 = (bf16[2,336,512]{2,1,0:T(8,128)(2,1)S(1)}, bf16[2,336,512]{2,1,0:T(8,128)(2,1)S(1)}, u32[]{:S(2)}, u32[]{:S(2)}) collective-permute-start(bf16[2,336,512]{2,1,0:T(8,128)(2,1)S(1)} %pad_maximum_fusion), channel_id=1, source_target_pairs={{0,2},{1,3},{2,0},{3,1},{4,6},{5,7},{6,4},{7,5},{8,10},{9,11},{10,... | collective-permute-start | bytes 2064392 | tf_op jit(solution)/shard_map/ppermute | solution.py:61
  28.7 23.2 %copy-start.17 = (bf16[4,144,384]{2,1,0:T(8,128)(2,1)}, bf16[4,144,384]{2,1,0:T(8,128)(2,1)S(1)}, u32[]{:S(2)}) copy-start(bf16[4,144,384]{2,1,0:T(8,128)(2,1)S(1)} %collective-permute-done.5.refs_5_) | copy-start | bytes 1327108
  36.7 11.4 %copy-start.18 = (bf16[4,144,384]{2,1,0:T(8,128)(2,1)}, bf16[4,144,384]{2,1,0:T(8,128)(2,1)S(1)}, u32[]{:S(2)}) copy-start(bf16[4,144,384]{2,1,0:T(8,128)(2,1)S(1)} %collective-permute-done.4.refs_3_) | copy-start | bytes 1327108
  36.7 12.0 %copy-start.19 = (bf16[4,144,384]{2,1,0:T(8,128)(2,1)}, bf16[4,144,384]{2,1,0:T(8,128)(2,1)S(1)}, u32[]{:S(2)}) copy-start(bf16[4,144,384]{2,1,0:T(8,128)(2,1)S(1)} %collective-permute-done.3.refs_2_) | copy-start | bytes 1327108
  36.7 9.7 %collective-permute-start.8 = (bf16[4,144,384]{2,1,0:T(8,128)(2,1)S(1)}, bf16[4,144,384]{2,1,0:T(8,128)(2,1)S(1)}, u32[]{:S(2)}, u32[]{:S(2)}) collective-permute-start(bf16[4,144,384]{2,1,0:T(8,128)(2,1)S(1)} %collective-permute-done.4.refs_3_), channel_id=1, source_target_pairs={{0,16},{16,0},{1,17},{17,1},{2,18},{18,2},{3,19},{19,3},{4,20},{20... | collective-permute-start | bytes 1327112 | tf_op jit(solution)/shard_map/ppermute | solution.py:57
  37.1 9.2 %collective-permute-start.7 = (bf16[4,144,384]{2,1,0:T(8,128)(2,1)S(1)}, bf16[4,144,384]{2,1,0:T(8,128)(2,1)S(1)}, u32[]{:S(2)}, u32[]{:S(2)}) collective-permute-start(bf16[4,144,384]{2,1,0:T(8,128)(2,1)S(1)} %collective-permute-done.3.refs_2_), channel_id=1, source_target_pairs={{0,16},{16,0},{1,17},{17,1},{2,18},{18,2},{3,19},{19,3},{4,20},{20... | collective-permute-start | bytes 1327112 | tf_op jit(solution)/shard_map/ppermute | solution.py:57
  37.2 10.7 %collective-permute-start.6 = (bf16[4,144,384]{2,1,0:T(8,128)(2,1)S(1)}, bf16[4,144,384]{2,1,0:T(8,128)(2,1)S(1)}, u32[]{:S(2)}, u32[]{:S(2)}) collective-permute-start(bf16[4,144,384]{2,1,0:T(8,128)(2,1)S(1)} %collective-permute-done.3.refs_2_), channel_id=1, source_target_pairs={{0,8},{1,9},{2,10},{3,11},{4,12},{5,13},{6,14},{7,15},{8,0},{9,1},... | collective-permute-start | bytes 1327112 | tf_op jit(solution)/shard_map/ppermute | solution.py:61
  47.9 1.3 copy-start.22
  48.0 14.9 %copy-start.8 = (bf16[4,336,512]{2,1,0:T(8,128)(2,1)}, bf16[4,336,512]{2,1,0:T(8,128)(2,1)S(1)}, u32[]{:S(2)}) copy-start(bf16[4,336,512]{2,1,0:T(8,128)(2,1)S(1)} %constant_dynamic-update-slice_fusion.refs_1_) | copy-start | bytes 4128772
  48.0 27.9 %collective-permute-start.12 = (bf16[4,336,512]{2,1,0:T(8,128)(2,1)S(1)}, bf16[4,336,512]{2,1,0:T(8,128)(2,1)S(1)}, u32[]{:S(2)}, u32[]{:S(2)}) collective-permute-start(bf16[4,336,512]{2,1,0:T(8,128)(2,1)S(1)} %constant_dynamic-update-slice_fusion.refs_1_), channel_id=1, source_target_pairs={{0,16},{16,0},{1,17},{17,1},{2,18},{18,2},{3,19},{19,3},{4,20},{20... | collective-permute-start | bytes 4128776 | tf_op jit(solution)/shard_map/ppermute | solution.py:57
  48.1 32.9 %collective-permute-start.11 = (bf16[4,336,512]{2,1,0:T(8,128)(2,1)S(1)}, bf16[4,336,512]{2,1,0:T(8,128)(2,1)}, u32[]{:S(2)}, u32[]{:S(2)}) collective-permute-start(bf16[4,336,512]{2,1,0:T(8,128)(2,1)S(1)} %constant_dynamic-update-slice_fusion.refs_1_), channel_id=1, source_target_pairs={{0,8},{1,9},{2,10},{3,11},{4,12},{5,13},{6,14},{7,15},{8,0},{9,1},... | collective-permute-start | bytes 4128776 | tf_op jit(solution)/shard_map/ppermute | solution.py:61
  48.6 32.4 %collective-permute-start.10 = (bf16[4,336,512]{2,1,0:T(8,128)(2,1)S(1)}, bf16[4,336,512]{2,1,0:T(8,128)(2,1)}, u32[]{:S(2)}, u32[]{:S(2)}) collective-permute-start(bf16[4,336,512]{2,1,0:T(8,128)(2,1)S(1)} %constant_dynamic-update-slice_fusion.refs_1_), channel_id=1, source_target_pairs={{0,4},{1,5},{2,6},{3,7},{4,0},{5,1},{6,2},{7,3},{8,12},{9,13},{10,... | collective-permute-start | bytes 4128776 | tf_op jit(solution)/shard_map/ppermute | solution.py:61
  49.2 2.8 collective-permute-start.13
  75.9 28.6 %copy-start.10 = (bf16[4,336,512]{2,1,0:T(8,128)(2,1)}, bf16[4,336,512]{2,1,0:T(8,128)(2,1)S(1)}, u32[]{:S(2)}) copy-start(bf16[4,336,512]{2,1,0:T(8,128)(2,1)S(1)} %collective-permute-done.12.refs_5_) | copy-start | bytes 4128772
  81.0 5.3 %collective-permute-start.16 = (bf16[4,336,512]{2,1,0:T(8,128)(2,1)}, bf16[4,336,512]{2,1,0:T(8,128)(2,1)S(1)}, u32[]{:S(2)}, u32[]{:S(2)}) collective-permute-start(bf16[4,336,512]{2,1,0:T(8,128)(2,1)} %collective-permute-done.11.refs_3_), channel_id=1, source_target_pairs={{0,16},{16,0},{1,17},{17,1},{2,18},{18,2},{3,19},{19,3},{4,20},{20... | collective-permute-start | bytes 4128776 | tf_op jit(solution)/shard_map/ppermute | solution.py:57
  81.0 5.4 %collective-permute-start.15 = (bf16[4,336,512]{2,1,0:T(8,128)(2,1)}, bf16[4,336,512]{2,1,0:T(8,128)(2,1)}, u32[]{:S(2)}, u32[]{:S(2)}) collective-permute-start(bf16[4,336,512]{2,1,0:T(8,128)(2,1)} %collective-permute-done.10.refs_2_), channel_id=1, source_target_pairs={{0,16},{16,0},{1,17},{17,1},{2,18},{18,2},{3,19},{19,3},{4,20},{20... | collective-permute-start | bytes 4128776 | tf_op jit(solution)/shard_map/ppermute | solution.py:57
  81.5 18.5 %collective-permute-start.14 = (bf16[4,336,512]{2,1,0:T(8,128)(2,1)}, bf16[4,336,512]{2,1,0:T(8,128)(2,1)S(1)}, u32[]{:S(2)}, u32[]{:S(2)}) collective-permute-start(bf16[4,336,512]{2,1,0:T(8,128)(2,1)} %collective-permute-done.10.refs_2_), channel_id=1, source_target_pairs={{0,8},{1,9},{2,10},{3,11},{4,12},{5,13},{6,14},{7,15},{8,0},{9,1},... | collective-permute-start | bytes 4128776 | tf_op jit(solution)/shard_map/ppermute | solution.py:61
  86.3 18.1 %copy-start.11 = (bf16[4,336,512]{2,1,0:T(8,128)(2,1)}, bf16[4,336,512]{2,1,0:T(8,128)(2,1)S(1)}, u32[]{:S(2)}) copy-start(bf16[4,336,512]{2,1,0:T(8,128)(2,1)S(1)} %collective-permute-done.16.refs_7_) | copy-start | bytes 4128772
  101.1 3.3 %collective-permute-start.17 = (bf16[4,336,512]{2,1,0:T(8,128)(2,1)S(1)}, bf16[4,336,512]{2,1,0:T(8,128)(2,1)}, u32[]{:S(2)}, u32[]{:S(2)}) collective-permute-start(bf16[4,336,512]{2,1,0:T(8,128)(2,1)S(1)} %collective-permute-done.14.refs_4_), channel_id=1, source_target_pairs={{0,16},{16,0},{1,17},{17,1},{2,18},{18,2},{3,19},{19,3},{4,20},{20... | collective-permute-start | bytes 4128776 | tf_op jit(solution)/shard_map/ppermute | solution.py:57
  157.2 10.6 %collective-permute-start.18 = (bf16[4,4,192,512]{3,2,1,0:T(8,128)(2,1)}, bf16[4,4,192,512]{3,2,1,0:T(8,128)(2,1)S(1)}, u32[]{:S(2)}, u32[]{:S(2)}) collective-permute-start(bf16[4,4,192,512]{3,2,1,0:T(8,128)(2,1)} %get-tuple-element.131), channel_id=1, source_target_pairs={{0,16},{16,0},{1,17},{17,1},{2,18},{18,2},{3,19},{19,3},{4,20},{20... | collective-permute-start | bytes 9437192 | tf_op jit(solution)/shard_map/ppermute | solution.py:57
  167.8 5.0 %copy-start = (bf16[4,4,192,512]{3,2,1,0:T(8,128)(2,1)}, bf16[4,4,192,512]{3,2,1,0:T(8,128)(2,1)S(1)}, u32[]{:S(2)}) copy-start(bf16[4,4,192,512]{3,2,1,0:T(8,128)(2,1)S(1)} %collective-permute-done.18.refs_1_) | copy-start | bytes 9437188
  167.8 4.9 %collective-permute-start.19 = (bf16[4,4,144,512]{3,2,1,0:T(8,128)(2,1)}, bf16[4,4,144,512]{3,2,1,0:T(8,128)(2,1)}, u32[]{:S(2)}, u32[]{:S(2)}) collective-permute-start(bf16[4,4,144,512]{3,2,1,0:T(8,128)(2,1)} %get-tuple-element.140), channel_id=1, source_target_pairs={{0,16},{16,0},{1,17},{17,1},{2,18},{18,2},{3,19},{19,3},{4,20},{20... | collective-permute-start | bytes 7077896 | tf_op jit(solution)/shard_map/ppermute | solution.py:57
  176.7 33.3 %collective-permute-start.20 = (bf16[2,4,336,512]{3,2,1,0:T(8,128)(2,1)}, bf16[2,4,336,512]{3,2,1,0:T(8,128)(2,1)S(1)}, u32[]{:S(2)}, u32[]{:S(2)}) collective-permute-start(bf16[2,4,336,512]{3,2,1,0:T(8,128)(2,1)} %sum_blocks.4), channel_id=1, source_target_pairs={{0,8},{1,9},{2,10},{3,11},{4,12},{5,13},{6,14},{7,15},{8,0},{9,1},... | collective-permute-start | bytes 8257544 | tf_op jit(solution)/shard_map/ppermute | solution.py:61
  210.0 1.6 copy-start.1
  214.8 18.5 %collective-permute-start.22 = (bf16[1,4,336,512]{3,2,1,0:T(8,128)(2,1)}, bf16[1,4,336,512]{3,2,1,0:T(8,128)(2,1)S(1)}, u32[]{:S(2)}, u32[]{:S(2)}) collective-permute-start(bf16[1,4,336,512]{3,2,1,0:T(8,128)(2,1)} %sum_blocks.5), channel_id=1, source_target_pairs={{0,4},{1,5},{2,6},{3,7},{4,0},{5,1},{6,2},{7,3},{8,12},{9,13},{10,... | collective-permute-start | bytes 4128776 | tf_op jit(solution)/shard_map/ppermute | solution.py:61
  227.8 2.6 collective-permute-start.21
  233.4 13.8 %collective-permute-start.23 = (bf16[2,4,144,384]{3,2,1,0:T(8,128)(2,1)}, bf16[2,4,144,384]{3,2,1,0:T(8,128)(2,1)S(1)}, u32[]{:S(2)}, u32[]{:S(2)}) collective-permute-start(bf16[2,4,144,384]{3,2,1,0:T(8,128)(2,1)} %slice_add_fusion), channel_id=1, source_target_pairs={{0,8},{1,9},{2,10},{3,11},{4,12},{5,13},{6,14},{7,15},{8,0},{9,1},... | collective-permute-start | bytes 2654216 | tf_op jit(solution)/shard_map/ppermute | solution.py:61
  233.8 13.3 %collective-permute-start.25 = (bf16[2,4,144,384]{3,2,1,0:T(8,128)(2,1)}, bf16[2,4,144,384]{3,2,1,0:T(8,128)(2,1)S(1)}, u32[]{:S(2)}, u32[]{:S(2)}) collective-permute-start(bf16[2,4,144,384]{3,2,1,0:T(8,128)(2,1)} %get-tuple-element.168), channel_id=1, source_target_pairs={{0,16},{16,0},{1,17},{17,1},{2,18},{18,2},{3,19},{19,3},{4,20},{20... | collective-permute-start | bytes 2654216 | tf_op jit(solution)/shard_map/ppermute | solution.py:57
  237.2 19.4 %collective-permute-start.24 = (bf16[1,2,336,512]{3,2,1,0:T(8,128)(2,1)}, bf16[1,2,336,512]{3,2,1,0:T(8,128)(2,1)S(1)}, u32[]{:S(2)}, u32[]{:S(2)}) collective-permute-start(bf16[1,2,336,512]{3,2,1,0:T(8,128)(2,1)} %sum_blocks.6), channel_id=1, source_target_pairs={{0,2},{1,3},{2,0},{3,1},{4,6},{5,7},{6,4},{7,5},{8,10},{9,11},{10,... | collective-permute-start | bytes 2064392 | tf_op jit(solution)/shard_map/ppermute | solution.py:61
  247.1 28.8 %copy-start.4 = (bf16[2,4,144,384]{3,2,1,0:T(8,128)(2,1)}, bf16[2,4,144,384]{3,2,1,0:T(8,128)(2,1)S(1)}, u32[]{:S(2)}) copy-start(bf16[2,4,144,384]{3,2,1,0:T(8,128)(2,1)S(1)} %collective-permute-done.23.refs_10_) | copy-start | bytes 2654212
  247.1 28.8 %copy-start.5 = (bf16[2,4,144,384]{3,2,1,0:T(8,128)(2,1)}, bf16[2,4,144,384]{3,2,1,0:T(8,128)(2,1)S(1)}, u32[]{:S(2)}) copy-start(bf16[2,4,144,384]{3,2,1,0:T(8,128)(2,1)S(1)} %collective-permute-done.25.refs_9_) | copy-start | bytes 2654212
  248.7 11.3 %collective-permute-start.26 = (bf16[1,4,144,384]{3,2,1,0:T(8,128)(2,1)S(1)}, bf16[1,4,144,384]{3,2,1,0:T(8,128)(2,1)S(1)}, u32[]{:S(2)}, u32[]{:S(2)}) collective-permute-start(bf16[1,4,144,384]{3,2,1,0:T(8,128)(2,1)S(1)} %add_convert_fusion), channel_id=1, source_target_pairs={{0,4},{1,5},{2,6},{3,7},{4,0},{5,1},{6,2},{7,3},{8,12},{9,13},{10,... | collective-permute-start | bytes 1327112 | tf_op jit(solution)/shard_map/ppermute | solution.py:61
  259.9 21.9 %copy-start.13 = (bf16[1,4,144,384]{3,2,1,0:T(8,128)(2,1)}, bf16[1,4,144,384]{3,2,1,0:T(8,128)(2,1)S(1)}, u32[]{:S(2)}) copy-start(bf16[1,4,144,384]{3,2,1,0:T(8,128)(2,1)S(1)} %collective-permute-done.26.refs_11_) | copy-start | bytes 1327108
  261.1 14.8 %collective-permute-start.27 = (bf16[1,2,144,384]{3,2,1,0:T(8,128)(2,1)S(1)}, bf16[1,2,144,384]{3,2,1,0:T(8,128)(2,1)S(1)}, u32[]{:S(2)}, u32[]{:S(2)}) collective-permute-start(bf16[1,2,144,384]{3,2,1,0:T(8,128)(2,1)S(1)} %add_convert_fusion.1), channel_id=1, source_target_pairs={{0,2},{1,3},{2,0},{3,1},{4,6},{5,7},{6,4},{7,5},{8,10},{9,11},{10,... | collective-permute-start | bytes 663560 | tf_op jit(solution)/shard_map/ppermute | solution.py:61
  261.6 20.2 %collective-permute-start.29 = (bf16[1,1,336,512]{3,2,1,0:T(8,128)(2,1)}, bf16[1,1,336,512]{3,2,1,0:T(8,128)(2,1)S(1)}, u32[]{:S(2)}, u32[]{:S(2)}) collective-permute-start(bf16[1,1,336,512]{3,2,1,0:T(8,128)(2,1)} %sum_blocks.7), channel_id=1, source_target_pairs={{0,1},{1,0},{2,3},{3,2},{4,5},{5,4},{6,7},{7,6},{8,9},{9,8},{10,11... | collective-permute-start | bytes 1032200 | tf_op jit(solution)/shard_map/ppermute | solution.py:61
  275.9 5.9 %copy-start.15 = (bf16[1,2,144,384]{3,2,1,0:T(8,128)(2,1)}, bf16[1,2,144,384]{3,2,1,0:T(8,128)(2,1)S(1)}, u32[]{:S(2)}) copy-start(bf16[1,2,144,384]{3,2,1,0:T(8,128)(2,1)S(1)} %collective-permute-done.27.refs_12_) | copy-start | bytes 663556
  277.0 4.8 %collective-permute-start.28 = (bf16[1,1,144,384]{3,2,1,0:T(8,128)(2,1)S(1)}, bf16[1,1,144,384]{3,2,1,0:T(8,128)(2,1)S(1)}, u32[]{:S(2)}, u32[]{:S(2)}) collective-permute-start(bf16[1,1,144,384]{3,2,1,0:T(8,128)(2,1)S(1)} %add_convert_fusion.2), channel_id=1, source_target_pairs={{0,1},{1,0},{2,3},{3,2},{4,5},{5,4},{6,7},{7,6},{8,9},{9,8},{10,11... | collective-permute-start | bytes 331784 | tf_op jit(solution)/shard_map/ppermute | solution.py:61
  286.0 2.1 collective-permute-start.30
  (8 other events, 6.8 us)
where the time goes:
time: 293 us; the launch traced here: 292 us
  Pallas kernels  160 us (55%)
  waiting for transfers between devices  84.1 us (29%)
  starting transfers between devices  22.9 us (8%)
  other arithmetic  12.6 us (4%)
  local copies, waits for them, and re-layouts  10.6 us (4%)
    ppermute x18, waiting for transfers between devices, exchange(): return lax.ppermute(value, EVERYWHERE, step_pairs(*grid, step))  64.4 us
    pallas_call x1, Pallas kernels, middle(): pl.pallas_call(lambda *refs: middle_body(grid, len(pieces), *refs), grid=...  41.2 us
    pallas_call x2, Pallas kernels, attention_backward(): pl.pallas_call(attention_backward_body, grid_spec=pltpu.PrefetchScalarGri...  29.7 us
    ppermute x18, starting transfers between devices, exchange(): return lax.ppermute(value, EVERYWHERE, step_pairs(*grid, step))  19.9 us
    ppermute x13, waiting for transfers between devices, other_core(): return lax.ppermute(value, 'dp', [(0, 1), (1, 0)])  19.7 us
    pallas_call x1, Pallas kernels, attention_forward(): pl.pallas_call(attention_forward_body, grid_spec=pltpu.PrefetchScalarGrid...  12.9 us
    pallas_call x1, Pallas kernels, attention_grads(): pl.pallas_call(lambda *refs: attention_grads_body(grid, *refs), grid_spec...  12.7 us
    pallas_call x4, Pallas kernels, sums(): pl.pallas_call(lambda *refs: sum_blocks_body(([len(part) for part in self...  12.3 us
  transfers between devices with their start and end apart: 31, of which 18 were waited for; matrix products, arithmetic and copies ran while one was open for 5% of the time, Pallas kernels for 32%

commit v1 on v0

--- a/solution.py
+++ b/solution.py
@@ -261,9 +261,10 @@
     out[rows, 256:384] = jnp.concatenate([low, high], axis=1).astype(BF16)
 
 
-def pack_attention_body(place, query, key, value, out):
+def pack_attention_body(query, key, value, out):
     half = query.shape[0] // 2
     quarter = half // 2
+    place = lax.axis_index("row"), lax.axis_index("col"), lax.axis_index("dp")
     odd = (place[1] & 1) == 1
     base = place[2] * half
     query, key = (w[pl.ds(pl.multiple_of(base, half), half), :].astype(F32) for w in (query, key))
@@ -272,17 +273,17 @@
     pack_pair(value[:quarter], value[quarter:], odd, out, slice(half, half + quarter))
 
 
-def pack_attention(place, query, key, value):
+def pack_attention(query, key, value):
     half = query.shape[0] // 2
     vmem = pl.BlockSpec(memory_space=pltpu.VMEM)
     return pl.pallas_call(
         pack_attention_body,
-        in_specs=[pl.BlockSpec(memory_space=pltpu.SMEM)] + [vmem] * 3,
+        in_specs=[vmem] * 3,
         out_specs=vmem,
         out_shape=jax.ShapeDtypeStruct((half + half // 2, 384), BF16),
         cost_estimate=costs(2),
         name="pack_attention",
-    )(place, query, key, value)
+    )(query, key, value)
 
 
 def pack_feed_body(place, gate, up, down, output, gain_one, gain_two, out):
@@ -426,25 +427,22 @@
     half = w_gate.shape[0] // grid_rows // 2
     quarter = half // 2
     span = w_gate.shape[1] // grid_cols
-    for piece, (side, at, count) in zip(pieces, piece_places(pieces)):
-        core = side ^ place[2]
-
-        @pl.loop(0, count)
-        def _(n):
-            row, col = block_at(at + n, place, core, grid)
-            block = piece.at[n]
-            rows = pl.ds(pl.multiple_of((2 * row + core) * half, half), half)
-            lanes = pl.ds(pl.multiple_of(col * span, span), span)
-            turned_rows = pl.ds(pl.multiple_of((2 * col + core) * half, half), half)
-            turned_lanes = pl.ds(pl.multiple_of(row * span, span), span)
-            parts = (
-                (0, 2 * half, quarter, held.at[side, at + n]),
-                (1, 0, half, w_gate.at[rows, lanes]),
-                (2, half, half, w_up.at[rows, lanes]),
-                (3, 2 * half + quarter, half, w_down.at[turned_rows, turned_lanes]),
-            )
-            for k, start, size, target in parts:
-                pltpu.make_async_copy(block.at[pl.ds(start, size)], target, sems.at[k]).start()
+    for k, (begin, size) in enumerate(((2 * half, quarter), (0, half), (half, half), (2 * half + quarter, half))):
+        for piece, (side, at, count) in zip(pieces, piece_places(pieces)):
+            core = side ^ place[2]
+
+            @pl.loop(0, count)
+            def _(n):
+                row, col = block_at(at + n, place, core, grid)
+                if k == 0:
+                    target = held.at[side, at + n]
+                elif k < 3:
+                    rows = pl.ds(pl.multiple_of((2 * row + core) * half, half), half)
+                    target = (w_gate, w_up)[k - 1].at[rows, pl.ds(pl.multiple_of(col * span, span), span)]
+                else:
+                    rows = pl.ds(pl.multiple_of((2 * col + core) * half, half), half)
+                    target = w_down.at[rows, pl.ds(pl.multiple_of(row * span, span), span)]
+                pltpu.make_async_copy(piece.at[n, pl.ds(begin, size)], target, sems.at[k]).start()
 
 
 def swap_halves(values):
@@ -824,21 +822,11 @@
     return jnp.where(core == 0, far, reversed_bits(far, bit_count(count)))
 
 
-def store_split(own, low, high, where, grid, core_here, row, col, rows, lanes, halves):
+def store_halves(own, other, where, grid, core_here, row, col, rows, lanes, halves):
     here = core_here == 0
-    at = part_of(row, where[0], core_here, grid[0]), part_of(col, where[1], core_here, grid[1])
-    own[at[0], at[1], rows, lanes] = jnp.where(here, halves[0], halves[1])
-    at = part_of(row, where[0], 1 - core_here, grid[0]), part_of(col, where[1], 1 - core_here, grid[1])
-    value = jnp.where(here, halves[1], halves[0])
-    edge = grid[0] // 2
-
-    @pl.when(at[0] < edge)
-    def _():
-        low[at[0], at[1], rows, lanes] = value
-
-    @pl.when(at[0] >= edge)
-    def _():
-        high[at[0] - edge, at[1], rows, lanes] = value
+    for target, core, first, second in ((own, core_here, 0, 1), (other, 1 - core_here, 1, 0)):
+        at = part_of(row, where[0], core, grid[0]), part_of(col, where[1], core, grid[1])
+        target[at[0], at[1], rows, lanes] = jnp.where(here, halves[first], halves[second])
 
 
 def rest_tile(first, second, odd):
@@ -956,7 +944,7 @@
     return own, other
 
 
-def attention_grads_body(grid, place, x_turned, grad_query, grad_key, grad_value, own, lower, upper):
+def attention_grads_body(grid, place, x_turned, grad_query, grad_key, grad_value, own, lower, upper, other, sems):
     grid_rows, grid_cols = grid
     where = (place[0], place[1])
     half = x_turned.shape[0] // grid_rows // 2
@@ -979,7 +967,19 @@
                 lanes = slice(128 * k, 128 * (k + 1))
                 at = (row, 2 * pair + odd)
                 for n, rows in ((k, slice(0, half)), (3 + k, slice(half, half + quarter))):
-                    store_split(own, lower, upper, where, grid, place[2], *at, rows, lanes, [p[n] for p in pieces])
+                    store_halves(own, other, where, grid, place[2], *at, rows, lanes, [p[n] for p in pieces])
+
+    @pl.when(pair == pl.num_programs(0) - 1)
+    def _():
+        edge = grid_rows // 2
+        copies = [
+            pltpu.make_async_copy(other.at[pl.ds(begin, edge)], target, sems.at[k])
+            for k, (begin, target) in enumerate(((edge, upper), (0, lower)))
+        ]
+        for copy in copies:
+            copy.start()
+        for copy in copies:
+            copy.wait()
 
 
 def attention_grads(place, grid, x_turned, grads):
@@ -988,7 +988,8 @@
     half = width // grid_rows // 2
     shape = (grid_rows, grid_cols, half + half // 2, 384)
     half_shape = (grid_rows // 2, *shape[1:])
-    out, part = (pl.BlockSpec(v, lambda i, s: (0, 0, 0, 0), pipeline_mode=pl.Buffered(1)) for v in (shape, half_shape))
+    out = pl.BlockSpec(shape, lambda i, s: (0, 0, 0, 0), pipeline_mode=pl.Buffered(1))
+    anywhere = pl.BlockSpec(memory_space=pl.ANY)
     return pl.pallas_call(
         lambda *refs: attention_grads_body(grid, *refs),
         grid_spec=pltpu.PrefetchScalarGridSpec(
@@ -996,7 +997,8 @@
             grid=(width // 384,),
             in_specs=[pl.BlockSpec((width, tokens), lambda i, s: (0, 0), pipeline_mode=pl.Buffered(1))]
             + [pl.BlockSpec((tokens, 384), lambda i, s: (0, i))] * 3,
-            out_specs=[out, part, part],
+            out_specs=[out, anywhere, anywhere],
+            scratch_shapes=[pltpu.VMEM(shape, BF16), pltpu.SemaphoreType.DMA((2,))],
         ),
         out_shape=[jax.ShapeDtypeStruct(v, BF16) for v in (shape, half_shape, half_shape)],
         cost_estimate=costs(8),
@@ -1108,12 +1110,12 @@
         )
 
     join = lambda *stacks: jnp.concatenate(stacks, axis=0)
-    q0 = pack_attention(place, query_weight, key_weight, value_weight)[None]
+    q0 = pack_attention(query_weight, key_weight, value_weight)[None]
     f0 = pack_feed(place, gate_weight, up_weight, down_weight.T, output_weight, first_gain, second_gain)[None]
     q1 = exchange(q0, grid, 0)
     f1 = exchange(f0, grid, 0)
-    q1, f0, segments, x_in = tie(q1, f0, segment_ids, inputs)
-    q01 = join(q0, q1)
+    q1, f0 = tie(q1, f0)
+    q01, segments, x_in = tie(join(q0, q1), segment_ids, inputs)
     q2 = exchange(q01, grid, 1)
     cosine, sine, first = tables(segments)
     x_turned = x_in.T
@@ -1144,19 +1146,24 @@
     ) = middle((f03, f3, f4, f5, f03_other, f3_other, f4_other, other_core(f5)), place, grid, context, inputs, cotangent)
 
     pairs = width // LANES
-    feed = Scatter(grid)
+    upper, lower, feed = Scatter(grid), Scatter(grid), Scatter(grid)
     own, other = feed_grads(place, grid, hidden_in_turned, (grad_gate, grad_up))
     other, branch_two_turned = tie(other, branch_two_turned)
     received = other_core(other)
     low_own, low_other = down_grads(place, grid, branch_two_turned, hidden, context_turned, branch_one, gain_grads)
     received, low_other = tie(received, low_other)
-    feed.add(own, received)
-    feed.add(low_own, other_core(low_other))
-    came = feed.send(feed.sums([2, 0], [2, 4]), 3)
+    low_received = other_core(low_other)
+    upper.add(own, received)
+    away, low_own = tie(upper.sums([2, 0], [2, 4]), low_own)
+    came = upper.send(away, 3)
+    lower.add(low_own, low_received)
+    away, grad_context = tie(lower.sums([2, 0], [2, 4]), grad_context)
+    low_came = lower.send(away, 3)
     grads = backward(grad_context, context, lse, 0, pairs // 2, ())
     grads = backward(grad_context, context, lse, pairs // 2, pairs // 2, grads)
-    came, x_turned, grads = tie(came, x_turned, grads)
-    feed.put(came)
+    came, low_came, x_turned, grads = tie(came, low_came, x_turned, grads)
+    feed.add(own, received, came)
+    feed.add(low_own, low_received, low_came)
     away, x_turned = tie(feed.sums([1, 0], [1, 4]), x_turned)
     came = feed.send(away, 2)
     heads = Scatter(grid)

time: 293 us -> 287 us (0.980)
  Pallas kernels: 160 us -> 153 us
  other arithmetic: 12.6 us -> 16.6 us
    add x1 -> x3, other arithmetic: 2.19 us -> 6.9 us  [sums(): return values[0] + values[1]]
    ppermute x13, waiting for transfers between devices: 19.7 us -> 15.5 us  [other_core(): return lax.ppermute(value, 'dp', [(0, 1), (1, 0)])]
    pallas_call x4 -> x3, Pallas kernels: 12.3 us -> 8.43 us  [sums(): pl.pallas_call(lambda *refs: sum_blocks_body(([len(part) for part in self...]
    ppermute x18 -> x19, waiting for transfers between devices: 64.4 us -> 66.9 us  [exchange(): return lax.ppermute(value, EVERYWHERE, step_pairs(*grid, step))]
    unnamed x52 -> x59, local copies, waits for them, and re-layouts: 7.57 us -> 8.15 us
    ppermute x18 -> x19, starting transfers between devices: 19.9 us -> 20.1 us  [exchange(): return lax.ppermute(value, EVERYWHERE, step_pairs(*grid, step))]
  transfers between devices with their start and end apart: 31 -> 32, of which waited for: 18 -> 18; matrix products, arithmetic and copies ran while one was open for 5% -> 6% of each run, Pallas kernels for 32% -> 32%
where the time goes in v1:
time: 287 us; the launch traced here: 286 us
  Pallas kernels  153 us (53%)
  waiting for transfers between devices  82.4 us (29%)
  starting transfers between devices  22.2 us (8%)
  other arithmetic  16.6 us (6%)
  local copies, waits for them, and re-layouts  10.5 us (4%)
    ppermute x19, waiting for transfers between devices, exchange(): return lax.ppermute(value, EVERYWHERE, step_pairs(*grid, step))  66.9 us
    pallas_call x1, Pallas kernels, middle(): pl.pallas_call(lambda *refs: middle_body(grid, len(pieces), *refs), grid=...  39.5 us
    pallas_call x2, Pallas kernels, attention_backward(): pl.pallas_call(attention_backward_body, grid_spec=pltpu.PrefetchScalarGri...  29.7 us
    ppermute x19, starting transfers between devices, exchange(): return lax.ppermute(value, EVERYWHERE, step_pairs(*grid, step))  20.1 us
    ppermute x13, waiting for transfers between devices, other_core(): return lax.ppermute(value, 'dp', [(0, 1), (1, 0)])  15.5 us
    pallas_call x1, Pallas kernels, attention_forward(): pl.pallas_call(attention_forward_body, grid_spec=pltpu.PrefetchScalarGrid...  13 us
    pallas_call x1, Pallas kernels, feed_grads(): pl.pallas_call(lambda *refs: feed_grads_body(grid, count, *refs), grid_sp...  11.6 us
    pallas_call x1, Pallas kernels, attention_grads(): pl.pallas_call(lambda *refs: attention_grads_body(grid, *refs), grid_spec...  11.4 us
  transfers between devices with their start and end apart: 32, of which 18 were waited for; matrix products, arithmetic and copies ran while one was open for 6% of the time, Pallas kernels for 32%

profile of v1, /device:TPU:0, one launch (start us, length us, event | category | flops | bytes accessed | tf_op | source)
XLA Modules:
  0.0 286.1 jit_solution(16888766536793633293)
XLA Ops:
  0.7 1.8 pack_attention.1
  2.4 3.0 %collective-permute-start = (bf16[1,144,384]{2,1,0:T(8,128)(2,1)}, bf16[1,144,384]{2,1,0:T(8,128)(2,1)S(1)}, u32[]{:S(2)}, u32[]{:S(2)}) collective-permute-start(bf16[1,144,384]{2,1,0:T(8,128)(2,1)} %bitcast.16), channel_id=1, source_target_pairs={{0,1},{1,0},{2,3},{3,2},{4,5},{5,4},{6,7},{7,6},{8,9},{9,8},{10,11... | collective-permute-start | bytes 331784 | tf_op jit(solution)/shard_map/ppermute | solution.py:61
  6.1 2.0 pack_feed.1
  8.1 1.4 collective-permute-done
  11.8 2.1 collective-permute-start.1
  13.9 1.9 fusion
  15.8 1.9 pad_maximum_fusion.1
  17.7 1.6 copy.28
  19.9 3.3 %collective-permute-done.1 = bf16[2,144,384]{2,1,0:T(8,128)(2,1)S(1)} collective-permute-done((bf16[2,144,384]{2,1,0:T(8,128)(2,1)S(1)}, bf16[2,144,384]{2,1,0:T(8,128)(2,1)S(1)}, u32[]{:S(2)}, u32[]{:S(2)}) %collective-permute-start.1) | collective-permute-done | bytes 221216 | tf_op jit(solution)/shard_map/ppermute | solution.py:61
  24.2 1.5 collective-permute-start.4
  25.7 1.5 collective-permute-start.3
  27.3 1.5 collective-permute-start.9
  28.7 7.9 %collective-permute-done.4.refs_3_ = bf16[4,144,384]{2,1,0:T(8,128)(2,1)S(1)} collective-permute-done((bf16[4,144,384]{2,1,0:T(8,128)(2,1)S(1)}, bf16[4,144,384]{2,1,0:T(8,128)(2,1)S(1)}, u32[]{:S(2)}, u32[]{:S(2)}) %collective-permute-start.4) | collective-permute-done | bytes 442400 | tf_op jit(solution)/shard_map/ppermute | solution.py:61
  37.3 1.5 collective-permute-start.6
  38.9 7.7 %collective-permute-done.9 = bf16[2,336,512]{2,1,0:T(8,128)(2,1)S(1)} collective-permute-done((bf16[2,336,512]{2,1,0:T(8,128)(2,1)S(1)}, bf16[2,336,512]{2,1,0:T(8,128)(2,1)S(1)}, u32[]{:S(2)}, u32[]{:S(2)}) %collective-permute-start.9) | collective-permute-done | bytes 688160 | tf_op jit(solution)/shard_map/ppermute | solution.py:61
  49.4 2.8 collective-permute-done.13.refs_8_
  52.2 10.9 %project_heads.1 = (bf16[1024,768]{1,0:T(8,128)(2,1)}, bf16[1024,768]{1,0:T(8,128)(2,1)}, bf16[1024,768]{1,0:T(8,128)(2,1)}, bf16[768,768]{1,0:T(8,128)(2,1)}, b...) custom-call(s32[3]{0:T(128)} %pad_add_fusion.place.refs_0_, bf16[4,144,384]{2,1,0:T(8,128)(2,1)} %copy-done.16, ...), custom_call_target="tpu_custom_call" | custom-call | flops 100000000 | bytes 100000 | tf_op jit(solution)/shard_map/project_heads/pallas_call | solution.py:488
  63.1 13.0 %attention_forward.1 = (bf16[1024,768]{1,0:T(8,128)(2,1)}, f32[6,8,1024]{2,1,0:T(8,128)}) custom-call(s32[4]{0:T(128)} %and_select_fusion.first, bf16[1024,768]{1,0:T(8,128)(2,1)} %get-tuple-element.120.q_ref, bf16[1024,768]{1,0:T(8,128)(2,1)} %get-tuple-element.121.k_ref, bf16[1024,768]{1,0:T(8,128)(2,1)} %get-tuple-element.122.v_ref), custom_call_target="tpu_custom_call" | custom-call | flops 240000000 | bytes 240000 | tf_op jit(solution)/shard_map/attention_forward/pallas_call | solution.py:568
  76.1 5.2 %collective-permute-done.11.refs_3_ = bf16[4,336,512]{2,1,0:T(8,128)(2,1)} collective-permute-done((bf16[4,336,512]{2,1,0:T(8,128)(2,1)S(1)}, bf16[4,336,512]{2,1,0:T(8,128)(2,1)}, u32[]{:S(2)}, u32[]{:S(2)}) %collective-permute-start.11) | collective-permute-done | bytes 1376288 | tf_op jit(solution)/shard_map/ppermute | solution.py:61
  82.3 4.2 %collective-permute-done.16.refs_7_ = bf16[4,336,512]{2,1,0:T(8,128)(2,1)S(1)} collective-permute-done((bf16[4,336,512]{2,1,0:T(8,128)(2,1)}, bf16[4,336,512]{2,1,0:T(8,128)(2,1)S(1)}, u32[]{:S(2)}, u32[]{:S(2)}) %collective-permute-start.16) | collective-permute-done | bytes 1376288 | tf_op jit(solution)/shard_map/ppermute | solution.py:57
  86.7 13.6 %collective-permute-done.14.refs_4_ = bf16[4,336,512]{2,1,0:T(8,128)(2,1)S(1)} collective-permute-done((bf16[4,336,512]{2,1,0:T(8,128)(2,1)}, bf16[4,336,512]{2,1,0:T(8,128)(2,1)S(1)}, u32[]{:S(2)}, u32[]{:S(2)}) %collective-permute-start.14) | collective-permute-done | bytes 1376288 | tf_op jit(solution)/shard_map/ppermute | solution.py:61
  100.3 1.1 copy-done.14
  101.4 3.3 %collective-permute-done.17.refs_8_ = bf16[4,336,512]{2,1,0:T(8,128)(2,1)} collective-permute-done((bf16[4,336,512]{2,1,0:T(8,128)(2,1)S(1)}, bf16[4,336,512]{2,1,0:T(8,128)(2,1)}, u32[]{:S(2)}, u32[]{:S(2)}) %collective-permute-start.17) | collective-permute-done | bytes 1376288 | tf_op jit(solution)/shard_map/ppermute | solution.py:57
  104.7 39.5 %feed_forward_and_back.1 = (bf16[1024,768]{1,0:T(8,128)(2,1)}, bf16[768,1024]{1,0:T(8,128)(2,1)}, bf16[768,1024]{1,0:T(8,128)(2,1)}, bf16[768,1024]{1,0:T(8,128)...) custom-call(s32[3]{0:T(128)} %pad_add_fusion.place.refs_0_, ...), custom_call_target="tpu_custom_call" | custom-call | flops 400000000 | bytes 400000 | tf_op jit(solution)/shard_map/feed_forward_and_back/pallas_call | solution.py:801
  144.2 11.6 %feed_forward_weight_grad.1 = (bf16[4,4,192,512]{3,2,1,0:T(8,128)(2,1)}, bf16[4,4,192,512]{3,2,1,0:T(8,128)(2,1)}) custom-call(s32[3]{0:T(128)} %pad_add_fusion.place.refs_0_, bf16[768,1024]{1,0:T(8,128)(2,1)} %get-tuple-element.132.refs_1_, bf16[1024,2048]{1,0:T(8,128)(2,1)} %get-tuple-element.133.refs_2_, bf16[1024,2048]{1,0:T(8,128)(2,1)} %get-tuple-element.134.refs_3_), custom_call_target="tpu_custom_call" | custom-call | flops 140000000 | bytes 140000 | tf_op jit(solution)/shard_map/feed_forward_weight_grad/pallas_call | solution.py:864
  155.9 10.4 %down_weight_grad.1 = (bf16[4,4,144,512]{3,2,1,0:T(8,128)(2,1)}, bf16[4,4,144,512]{3,2,1,0:T(8,128)(2,1)}) custom-call(s32[3]{0:T(128)} %pad_add_fusion.place.refs_0_, bf16[768,1024]{1,0:T(8,128)(2,1)} %get-tuple-element.139.refs_1_, bf16[1024,2048]{1,0:T(8,128)(2,1)} %get-tuple-element.140.refs_2_, bf16[768,1024]{1,0:T(8,128)(2,1)} %get-tuple-element.141.refs_3_, ...), custom_call_target="tpu_custom_call" | custom-call | flops 100000000 | bytes 100000 | tf_op jit(solution)/shard_map/down_weight_grad/pallas_call | solution.py:926
  166.7 3.4 %slice_add_fusion = bf16[2,4,192,512]{3,2,1,0:T(8,128)(2,1)} fusion(bf16[4,4,192,512]{3,2,1,0:T(8,128)(2,1)S(1)} %collective-permute-done.18.refs_1_, bf16[4,4,192,512]{3,2,1,0:T(8,128)(2,1)} %get-tuple-element.135.refs_0_), kind=kLoop, calls=%fused_computation | loop fusion | flops 786432 | bytes 4718592 | tf_op jit(solution)/shard_map/add | solution.py:116
  171.1 1.3 slice_add_fusion.1
  174.1 14.9 %attention_backward.2 = (bf16[1024,768]{1,0:T(8,128)(2,1)}, bf16[1024,768]{1,0:T(8,128)(2,1)}, bf16[1024,768]{1,0:T(8,128)(2,1)}) custom-call(s32[4]{0:T(128)} %and_select_fusion.first, bf16[1024,768]{1,0:T(8,128)(2,1)} %get-tuple-element.120.q_ref, bf16[1024,768]{1,0:T(8,128)(2,1)} %get-tuple-element.121.k_ref, bf16[1024,768]{1,0:T(8,128)(2,1)} %get-tuple-element.122.v_ref, ...), custom_call_target="tpu_custom_call" | custom-call | flops 180000000 | bytes 180000 | tf_op jit(solution)/shard_map/attention_backward/pallas_call | solution.py:642
  189.0 14.8 %attention_backward.3 = (bf16[1024,768]{1,0:T(8,128)(2,1)}, bf16[1024,768]{1,0:T(8,128)(2,1)}, bf16[1024,768]{1,0:T(8,128)(2,1)}) custom-call(s32[4]{0:T(128)} %and_select_fusion.first, bf16[1024,768]{1,0:T(8,128)(2,1)} %get-tuple-element.120.q_ref, ...), custom_call_target="tpu_custom_call", output_to_operand_aliasing={{0}: (9, {}), {1}: (10, {}), {2}: (11, {})} | custom-call | flops 180000000 | bytes 180000 | tf_op jit(solution)/shard_map/attention_backward/pallas_call | solution.py:642
  203.8 1.2 copy-done.3
  205.4 3.2 %sum_blocks.3 = bf16[1,4,336,512]{3,2,1,0:T(8,128)(2,1)} custom-call(bf16[4,4,192,512]{3,2,1,0:T(8,128)(2,1)} %get-tuple-element.135.refs_0_, bf16[4,4,192,512]{3,2,1,0:T(8,128)(2,1)} %copy-done, bf16[2,4,192,512]{3,2,1,0:T(8,128)(2,1)} %copy-done.3, bf16[4,4,144,512]{3,2,1,0:T(8,128)(2,1)} %get-tuple-element.148.refs_3_, ...), custom_call_target="tpu_custom_call" | custom-call | flops 20000000 | bytes 20000 | tf_op jit(solution)/shard_map/sum_blocks/pallas_call | solution.py:128
  208.9 11.4 %attention_weight_grads.1 = (bf16[4,4,144,384]{3,2,1,0:T(8,128)(2,1)}, bf16[2,4,144,384]{3,2,1,0:T(8,128)(2,1)}, bf16[2,4,144,384]{3,2,1,0:T(8,128)(2,1)}) custom-call(s32[3]{0:T(128)} %pad_add_fusion.place.refs_0_, bf16[768,1024]{1,0:T(8,128)(2,1)} %bitcast.12, bf16[1024,768]{1,0:T(8,128)(2,1)} %get-tuple-element.165.refs_2_.grad_query, ...), custom_call_target="tpu_custom_call" | custom-call | flops 80000000 | bytes 80000 | tf_op jit(solution)/shard_map/attention_weight_grads/pallas_call | solution.py:993
  220.4 2.6 collective-permute-done.22
  223.0 2.2 slice_add_fusion.2
  225.2 1.9 collective-permute-done.23.refs_6_
  228.2 2.7 sum_blocks.4
  231.9 8.6 %input_gradient.1 = bf16[1024,768]{1,0:T(8,128)(2,1)} custom-call(f32[1024,768]{1,0:T(8,128)} %get-tuple-element.174.grad_first, bf16[1024,768]{1,0:T(8,128)(2,1)} %get-tuple-element.165.refs_2_.grad_query, bf16[1024,768]{1,0:T(8,128)(2,1)} %get-tuple-element.166.refs_3_.grad_key, bf16[1024,768]{1,0:T(8,128)(2,1)} %get-tuple-element.167.refs_4_.grad_value, ...), custom_call_target="tpu_custom_call" | custom-call | flops 80000000 | bytes 80000 | tf_op jit(solution)/shard_map/input_gradient/pallas_call | solution.py:1021
  240.5 1.5 add_convert_fusion
  242.5 7.5 %collective-permute-done.25.refs_7_ = bf16[1,2,336,512]{3,2,1,0:T(8,128)(2,1)S(1)} collective-permute-done((bf16[1,2,336,512]{3,2,1,0:T(8,128)(2,1)}, bf16[1,2,336,512]{3,2,1,0:T(8,128)(2,1)S(1)}, u32[]{:S(2)}, u32[]{:S(2)}) %collective-permute-start.25) | collective-permute-done | bytes 688160 | tf_op jit(solution)/shard_map/ppermute | solution.py:61
  250.9 2.5 sum_blocks.5
  253.3 1.2 add_convert_fusion.1
  254.8 2.8 collective-permute-start.30
  257.6 12.9 %collective-permute-done.28.refs_13_ = bf16[1,2,144,384]{3,2,1,0:T(8,128)(2,1)S(1)} collective-permute-done((bf16[1,2,144,384]{3,2,1,0:T(8,128)(2,1)S(1)}, bf16[1,2,144,384]{3,2,1,0:T(8,128)(2,1)S(1)}, u32[]{:S(2)}, u32[]{:S(2)}) %collective-permute-start.28) | collective-permute-done | bytes 221216 | tf_op jit(solution)/shard_map/ppermute | solution.py:61
  271.6 4.7 %collective-permute-done.29.refs_14_ = bf16[1,1,144,384]{3,2,1,0:T(8,128)(2,1)S(1)} collective-permute-done((bf16[1,1,144,384]{3,2,1,0:T(8,128)(2,1)S(1)}, bf16[1,1,144,384]{3,2,1,0:T(8,128)(2,1)S(1)}, u32[]{:S(2)}, u32[]{:S(2)}) %collective-permute-start.29) | collective-permute-done | bytes 110624 | tf_op jit(solution)/shard_map/ppermute | solution.py:61
  277.8 2.9 %last_sums.1.mine = bf16[480,512]{1,0:T(8,128)(2,1)} custom-call(bf16[4,4,192,512]{3,2,1,0:T(8,128)(2,1)} %get-tuple-element.135.refs_0_, bf16[4,4,192,512]{3,2,1,0:T(8,128)(2,1)} %copy-done, bf16[2,4,192,512]{3,2,1,0:T(8,128)(2,1)} %copy-done.3, bf16[4,4,144,512]{3,2,1,0:T(8,128)(2,1)} %get-tuple-element.148.refs_3_, bf16[4,4,144,512]{3,2,1,0:T(8,128)(2,1)} %copy-done.2, ...), custom_call_target="tpu_custom_call" | custom-call | flops 20000000 | bytes 20000 | tf_op jit(solution)/shard_map/last_sums/pallas_call | solution.py:175
  280.7 2.1 collective-permute-done.31.theirs
  283.5 2.6 finish.1
  (110 shorter events, 19.5 us)
Async XLA Ops:
  0.6 9.8 %copy-start.27 = (s32[1024]{0:T(1024)S(1)}, s32[1024]{0:T(1024)}, u32[]{:S(2)}) copy-start(s32[1024]{0:T(1024)} %param.13) | copy-start | bytes 12292
  2.4 7.1 %collective-permute-start = (bf16[1,144,384]{2,1,0:T(8,128)(2,1)}, bf16[1,144,384]{2,1,0:T(8,128)(2,1)S(1)}, u32[]{:S(2)}, u32[]{:S(2)}) collective-permute-start(bf16[1,144,384]{2,1,0:T(8,128)(2,1)} %bitcast.16), channel_id=1, source_target_pairs={{0,1},{1,0},{2,3},{3,2},{4,5},{5,4},{6,7},{7,6},{8,9},{9,8},{10,11... | collective-permute-start | bytes 331784 | tf_op jit(solution)/shard_map/ppermute | solution.py:61
  8.1 15.8 %collective-permute-start.2 = (bf16[1,336,512]{2,1,0:T(8,128)(2,1)}, bf16[1,336,512]{2,1,0:T(8,128)(2,1)S(1)}, u32[]{:S(2)}, u32[]{:S(2)}) collective-permute-start(bf16[1,336,512]{2,1,0:T(8,128)(2,1)} %bitcast.13), channel_id=1, source_target_pairs={{0,1},{1,0},{2,3},{3,2},{4,5},{5,4},{6,7},{7,6},{8,9},{9,8},{10,11... | collective-permute-start | bytes 1032200 | tf_op jit(solution)/shard_map/ppermute | solution.py:61
  11.8 11.3 %collective-permute-start.1 = (bf16[2,144,384]{2,1,0:T(8,128)(2,1)S(1)}, bf16[2,144,384]{2,1,0:T(8,128)(2,1)S(1)}, u32[]{:S(2)}, u32[]{:S(2)}) collective-permute-start(bf16[2,144,384]{2,1,0:T(8,128)(2,1)S(1)} %pad_maximum_fusion.3), channel_id=1, source_target_pairs={{0,2},{1,3},{2,0},{3,1},{4,6},{5,7},{6,4},{7,5},{8,10},{9,11},{10,... | collective-permute-start | bytes 663560 | tf_op jit(solution)/shard_map/ppermute | solution.py:61
  15.8 1.9 copy-start.5
  17.7 9.5 %copy-start.9 = (bf16[336,512]{1,0:T(8,128)(2,1)S(1)}, bf16[336,512]{1,0:T(8,128)(2,1)}, u32[]{:S(2)}) copy-start(bf16[336,512]{1,0:T(8,128)(2,1)} %pack_feed.1) | copy-start | bytes 1032196
  24.0 24.2 %copy-start.16 = (bf16[4,144,384]{2,1,0:T(8,128)(2,1)}, bf16[4,144,384]{2,1,0:T(8,128)(2,1)S(1)}, u32[]{:S(2)}) copy-start(bf16[4,144,384]{2,1,0:T(8,128)(2,1)S(1)} %constant_dynamic-update-slice_fusion.refs_1_) | copy-start | bytes 1327108
  24.0 4.7 %collective-permute-start.5 = (bf16[4,144,384]{2,1,0:T(8,128)(2,1)S(1)}, bf16[4,144,384]{2,1,0:T(8,128)(2,1)S(1)}, u32[]{:S(2)}, u32[]{:S(2)}) collective-permute-start(bf16[4,144,384]{2,1,0:T(8,128)(2,1)S(1)} %constant_dynamic-update-slice_fusion.refs_1_), channel_id=1, source_target_pairs={{0,16},{16,0},{1,17},{17,1},{2,18},{18,2},{3,19},{19,3},{4,20},{20... | collective-permute-start | bytes 1327112 | tf_op jit(solution)/shard_map/ppermute | solution.py:57
  24.2 12.5 %collective-permute-start.4 = (bf16[4,144,384]{2,1,0:T(8,128)(2,1)S(1)}, bf16[4,144,384]{2,1,0:T(8,128)(2,1)S(1)}, u32[]{:S(2)}, u32[]{:S(2)}) collective-permute-start(bf16[4,144,384]{2,1,0:T(8,128)(2,1)S(1)} %constant_dynamic-update-slice_fusion.refs_1_), channel_id=1, source_target_pairs={{0,8},{1,9},{2,10},{3,11},{4,12},{5,13},{6,14},{7,15},{8,0},{9,1},... | collective-permute-start | bytes 1327112 | tf_op jit(solution)/shard_map/ppermute | solution.py:61
  25.7 11.0 %collective-permute-start.3 = (bf16[4,144,384]{2,1,0:T(8,128)(2,1)S(1)}, bf16[4,144,384]{2,1,0:T(8,128)(2,1)S(1)}, u32[]{:S(2)}, u32[]{:S(2)}) collective-permute-start(bf16[4,144,384]{2,1,0:T(8,128)(2,1)S(1)} %constant_dynamic-update-slice_fusion.refs_1_), channel_id=1, source_target_pairs={{0,4},{1,5},{2,6},{3,7},{4,0},{5,1},{6,2},{7,3},{8,12},{9,13},{10,... | collective-permute-start | bytes 1327112 | tf_op jit(solution)/shard_map/ppermute | solution.py:61
  27.3 19.3 %collective-permute-start.9 = (bf16[2,336,512]{2,1,0:T(8,128)(2,1)S(1)}, bf16[2,336,512]{2,1,0:T(8,128)(2,1)S(1)}, u32[]{:S(2)}, u32[]{:S(2)}) collective-permute-start(bf16[2,336,512]{2,1,0:T(8,128)(2,1)S(1)} %pad_maximum_fusion), channel_id=1, source_target_pairs={{0,2},{1,3},{2,0},{3,1},{4,6},{5,7},{6,4},{7,5},{8,10},{9,11},{10,... | collective-permute-start | bytes 2064392 | tf_op jit(solution)/shard_map/ppermute | solution.py:61
  28.7 23.5 %copy-start.19 = (bf16[4,144,384]{2,1,0:T(8,128)(2,1)}, bf16[4,144,384]{2,1,0:T(8,128)(2,1)S(1)}, u32[]{:S(2)}) copy-start(bf16[4,144,384]{2,1,0:T(8,128)(2,1)S(1)} %collective-permute-done.5.refs_5_) | copy-start | bytes 1327108
  36.6 11.5 %copy-start.20 = (bf16[4,144,384]{2,1,0:T(8,128)(2,1)}, bf16[4,144,384]{2,1,0:T(8,128)(2,1)S(1)}, u32[]{:S(2)}) copy-start(bf16[4,144,384]{2,1,0:T(8,128)(2,1)S(1)} %collective-permute-done.4.refs_3_) | copy-start | bytes 1327108
  36.6 11.6 %copy-start.21 = (bf16[4,144,384]{2,1,0:T(8,128)(2,1)}, bf16[4,144,384]{2,1,0:T(8,128)(2,1)S(1)}, u32[]{:S(2)}) copy-start(bf16[4,144,384]{2,1,0:T(8,128)(2,1)S(1)} %collective-permute-done.3.refs_2_) | copy-start | bytes 1327108
  36.6 9.9 %collective-permute-start.8 = (bf16[4,144,384]{2,1,0:T(8,128)(2,1)S(1)}, bf16[4,144,384]{2,1,0:T(8,128)(2,1)S(1)}, u32[]{:S(2)}, u32[]{:S(2)}) collective-permute-start(bf16[4,144,384]{2,1,0:T(8,128)(2,1)S(1)} %collective-permute-done.4.refs_3_), channel_id=1, source_target_pairs={{0,16},{16,0},{1,17},{17,1},{2,18},{18,2},{3,19},{19,3},{4,20},{20... | collective-permute-start | bytes 1327112 | tf_op jit(solution)/shard_map/ppermute | solution.py:57
  37.3 9.2 %collective-permute-start.7 = (bf16[4,144,384]{2,1,0:T(8,128)(2,1)S(1)}, bf16[4,144,384]{2,1,0:T(8,128)(2,1)S(1)}, u32[]{:S(2)}, u32[]{:S(2)}) collective-permute-start(bf16[4,144,384]{2,1,0:T(8,128)(2,1)S(1)} %collective-permute-done.3.refs_2_), channel_id=1, source_target_pairs={{0,16},{16,0},{1,17},{17,1},{2,18},{18,2},{3,19},{19,3},{4,20},{20... | collective-permute-start | bytes 1327112 | tf_op jit(solution)/shard_map/ppermute | solution.py:57
  37.3 10.8 %collective-permute-start.6 = (bf16[4,144,384]{2,1,0:T(8,128)(2,1)S(1)}, bf16[4,144,384]{2,1,0:T(8,128)(2,1)S(1)}, u32[]{:S(2)}, u32[]{:S(2)}) collective-permute-start(bf16[4,144,384]{2,1,0:T(8,128)(2,1)S(1)} %collective-permute-done.3.refs_2_), channel_id=1, source_target_pairs={{0,8},{1,9},{2,10},{3,11},{4,12},{5,13},{6,14},{7,15},{8,0},{9,1},... | collective-permute-start | bytes 1327112 | tf_op jit(solution)/shard_map/ppermute | solution.py:61
  48.2 14.9 %copy-start.11 = (bf16[4,336,512]{2,1,0:T(8,128)(2,1)}, bf16[4,336,512]{2,1,0:T(8,128)(2,1)S(1)}, u32[]{:S(2)}) copy-start(bf16[4,336,512]{2,1,0:T(8,128)(2,1)S(1)} %constant_dynamic-update-slice_fusion.2.refs_1_) | copy-start | bytes 4128772
  48.2 27.9 %collective-permute-start.12 = (bf16[4,336,512]{2,1,0:T(8,128)(2,1)S(1)}, bf16[4,336,512]{2,1,0:T(8,128)(2,1)S(1)}, u32[]{:S(2)}, u32[]{:S(2)}) collective-permute-start(bf16[4,336,512]{2,1,0:T(8,128)(2,1)S(1)} %constant_dynamic-update-slice_fusion.2.refs_1_), channel_id=1, source_target_pairs={{0,16},{16,0},{1,17},{17,1},{2,18},{18,2},{3,19},{19,3},{4,20},{20... | collective-permute-start | bytes 4128776 | tf_op jit(solution)/shard_map/ppermute | solution.py:57
  48.3 32.9 %collective-permute-start.11 = (bf16[4,336,512]{2,1,0:T(8,128)(2,1)S(1)}, bf16[4,336,512]{2,1,0:T(8,128)(2,1)}, u32[]{:S(2)}, u32[]{:S(2)}) collective-permute-start(bf16[4,336,512]{2,1,0:T(8,128)(2,1)S(1)} %constant_dynamic-update-slice_fusion.2.refs_1_), channel_id=1, source_target_pairs={{0,8},{1,9},{2,10},{3,11},{4,12},{5,13},{6,14},{7,15},{8,0},{9,1},... | collective-permute-start | bytes 4128776 | tf_op jit(solution)/shard_map/ppermute | solution.py:61
  48.9 32.4 %collective-permute-start.10 = (bf16[4,336,512]{2,1,0:T(8,128)(2,1)S(1)}, bf16[4,336,512]{2,1,0:T(8,128)(2,1)}, u32[]{:S(2)}, u32[]{:S(2)}) collective-permute-start(bf16[4,336,512]{2,1,0:T(8,128)(2,1)S(1)} %constant_dynamic-update-slice_fusion.2.refs_1_), channel_id=1, source_target_pairs={{0,4},{1,5},{2,6},{3,7},{4,0},{5,1},{6,2},{7,3},{8,12},{9,13},{10,... | collective-permute-start | bytes 4128776 | tf_op jit(solution)/shard_map/ppermute | solution.py:61
  49.4 2.8 collective-permute-start.13
  76.1 28.6 %copy-start.12 = (bf16[4,336,512]{2,1,0:T(8,128)(2,1)}, bf16[4,336,512]{2,1,0:T(8,128)(2,1)S(1)}, u32[]{:S(2)}) copy-start(bf16[4,336,512]{2,1,0:T(8,128)(2,1)S(1)} %collective-permute-done.12.refs_5_) | copy-start | bytes 4128772
  81.2 5.3 %collective-permute-start.16 = (bf16[4,336,512]{2,1,0:T(8,128)(2,1)}, bf16[4,336,512]{2,1,0:T(8,128)(2,1)S(1)}, u32[]{:S(2)}, u32[]{:S(2)}) collective-permute-start(bf16[4,336,512]{2,1,0:T(8,128)(2,1)} %collective-permute-done.11.refs_3_), channel_id=1, source_target_pairs={{0,16},{16,0},{1,17},{17,1},{2,18},{18,2},{3,19},{19,3},{4,20},{20... | collective-permute-start | bytes 4128776 | tf_op jit(solution)/shard_map/ppermute | solution.py:57
  81.2 5.4 %collective-permute-start.15 = (bf16[4,336,512]{2,1,0:T(8,128)(2,1)}, bf16[4,336,512]{2,1,0:T(8,128)(2,1)}, u32[]{:S(2)}, u32[]{:S(2)}) collective-permute-start(bf16[4,336,512]{2,1,0:T(8,128)(2,1)} %collective-permute-done.10.refs_2_), channel_id=1, source_target_pairs={{0,16},{16,0},{1,17},{17,1},{2,18},{18,2},{3,19},{19,3},{4,20},{20... | collective-permute-start | bytes 4128776 | tf_op jit(solution)/shard_map/ppermute | solution.py:57
  81.7 18.5 %collective-permute-start.14 = (bf16[4,336,512]{2,1,0:T(8,128)(2,1)}, bf16[4,336,512]{2,1,0:T(8,128)(2,1)S(1)}, u32[]{:S(2)}, u32[]{:S(2)}) collective-permute-start(bf16[4,336,512]{2,1,0:T(8,128)(2,1)} %collective-permute-done.10.refs_2_), channel_id=1, source_target_pairs={{0,8},{1,9},{2,10},{3,11},{4,12},{5,13},{6,14},{7,15},{8,0},{9,1},... | collective-permute-start | bytes 4128776 | tf_op jit(solution)/shard_map/ppermute | solution.py:61
  86.5 18.2 %copy-start.13 = (bf16[4,336,512]{2,1,0:T(8,128)(2,1)}, bf16[4,336,512]{2,1,0:T(8,128)(2,1)S(1)}, u32[]{:S(2)}) copy-start(bf16[4,336,512]{2,1,0:T(8,128)(2,1)S(1)} %collective-permute-done.16.refs_7_) | copy-start | bytes 4128772
  101.4 3.3 %collective-permute-start.17 = (bf16[4,336,512]{2,1,0:T(8,128)(2,1)S(1)}, bf16[4,336,512]{2,1,0:T(8,128)(2,1)}, u32[]{:S(2)}, u32[]{:S(2)}) collective-permute-start(bf16[4,336,512]{2,1,0:T(8,128)(2,1)S(1)} %collective-permute-done.14.refs_4_), channel_id=1, source_target_pairs={{0,16},{16,0},{1,17},{17,1},{2,18},{18,2},{3,19},{19,3},{4,20},{20... | collective-permute-start | bytes 4128776 | tf_op jit(solution)/shard_map/ppermute | solution.py:57
  155.7 10.6 %collective-permute-start.18 = (bf16[4,4,192,512]{3,2,1,0:T(8,128)(2,1)}, bf16[4,4,192,512]{3,2,1,0:T(8,128)(2,1)S(1)}, u32[]{:S(2)}, u32[]{:S(2)}) collective-permute-start(bf16[4,4,192,512]{3,2,1,0:T(8,128)(2,1)} %get-tuple-element.138), channel_id=1, source_target_pairs={{0,16},{16,0},{1,17},{17,1},{2,18},{18,2},{3,19},{19,3},{4,20},{20... | collective-permute-start | bytes 9437192 | tf_op jit(solution)/shard_map/ppermute | solution.py:57
  166.3 3.9 %copy-start = (bf16[4,4,192,512]{3,2,1,0:T(8,128)(2,1)}, bf16[4,4,192,512]{3,2,1,0:T(8,128)(2,1)S(1)}, u32[]{:S(2)}) copy-start(bf16[4,4,192,512]{3,2,1,0:T(8,128)(2,1)S(1)} %collective-permute-done.18.refs_1_) | copy-start | bytes 9437188
  166.3 4.8 %collective-permute-start.20 = (bf16[4,4,144,512]{3,2,1,0:T(8,128)(2,1)}, bf16[4,4,144,512]{3,2,1,0:T(8,128)(2,1)S(1)}, u32[]{:S(2)}, u32[]{:S(2)}) collective-permute-start(bf16[4,4,144,512]{3,2,1,0:T(8,128)(2,1)} %get-tuple-element.149), channel_id=1, source_target_pairs={{0,16},{16,0},{1,17},{17,1},{2,18},{18,2},{3,19},{19,3},{4,20},{20... | collective-permute-start | bytes 7077896 | tf_op jit(solution)/shard_map/ppermute | solution.py:57
  166.7 4.4 %copy-start.1 = (bf16[4,4,144,512]{3,2,1,0:T(8,128)(2,1)S(1)}, bf16[4,4,144,512]{3,2,1,0:T(8,128)(2,1)}, u32[]{:S(2)}) copy-start(bf16[4,4,144,512]{3,2,1,0:T(8,128)(2,1)} %get-tuple-element.148.refs_3_) | copy-start | bytes 7077892
  170.2 33.6 %collective-permute-start.19 = (bf16[2,4,192,512]{3,2,1,0:T(8,128)(2,1)}, bf16[2,4,192,512]{3,2,1,0:T(8,128)(2,1)S(1)}, u32[]{:S(2)}, u32[]{:S(2)}) collective-permute-start(bf16[2,4,192,512]{3,2,1,0:T(8,128)(2,1)} %slice_add_fusion), channel_id=1, source_target_pairs={{0,8},{1,9},{2,10},{3,11},{4,12},{5,13},{6,14},{7,15},{8,0},{9,1},... | collective-permute-start | bytes 4718600 | tf_op jit(solution)/shard_map/ppermute | solution.py:61
  173.0 30.8 %collective-permute-start.21 = (bf16[2,4,144,512]{3,2,1,0:T(8,128)(2,1)}, bf16[2,4,144,512]{3,2,1,0:T(8,128)(2,1)S(1)}, u32[]{:S(2)}, u32[]{:S(2)}) collective-permute-start(bf16[2,4,144,512]{3,2,1,0:T(8,128)(2,1)} %slice_add_fusion.1), channel_id=1, source_target_pairs={{0,8},{1,9},{2,10},{3,11},{4,12},{5,13},{6,14},{7,15},{8,0},{9,1},... | collective-permute-start | bytes 3538952 | tf_op jit(solution)/shard_map/ppermute | solution.py:61
  208.6 18.5 %collective-permute-start.23 = (bf16[1,4,336,512]{3,2,1,0:T(8,128)(2,1)}, bf16[1,4,336,512]{3,2,1,0:T(8,128)(2,1)S(1)}, u32[]{:S(2)}, u32[]{:S(2)}) collective-permute-start(bf16[1,4,336,512]{3,2,1,0:T(8,128)(2,1)} %sum_blocks.3), channel_id=1, source_target_pairs={{0,4},{1,5},{2,6},{3,7},{4,0},{5,1},{6,2},{7,3},{8,12},{9,13},{10,... | collective-permute-start | bytes 4128776 | tf_op jit(solution)/shard_map/ppermute | solution.py:61
  220.3 2.7 collective-permute-start.22
  227.1 13.4 %collective-permute-start.24 = (bf16[2,4,144,384]{3,2,1,0:T(8,128)(2,1)}, bf16[2,4,144,384]{3,2,1,0:T(8,128)(2,1)S(1)}, u32[]{:S(2)}, u32[]{:S(2)}) collective-permute-start(bf16[2,4,144,384]{3,2,1,0:T(8,128)(2,1)} %slice_add_fusion.2), channel_id=1, source_target_pairs={{0,8},{1,9},{2,10},{3,11},{4,12},{5,13},{6,14},{7,15},{8,0},{9,1},... | collective-permute-start | bytes 2654216 | tf_op jit(solution)/shard_map/ppermute | solution.py:61
  228.1 12.5 %collective-permute-start.26 = (bf16[2,4,144,384]{3,2,1,0:T(8,128)(2,1)}, bf16[2,4,144,384]{3,2,1,0:T(8,128)(2,1)S(1)}, u32[]{:S(2)}, u32[]{:S(2)}) collective-permute-start(bf16[2,4,144,384]{3,2,1,0:T(8,128)(2,1)} %get-tuple-element.180), channel_id=1, source_target_pairs={{0,16},{16,0},{1,17},{17,1},{2,18},{18,2},{3,19},{19,3},{4,20},{20... | collective-permute-start | bytes 2654216 | tf_op jit(solution)/shard_map/ppermute | solution.py:57
  230.9 19.1 %collective-permute-start.25 = (bf16[1,2,336,512]{3,2,1,0:T(8,128)(2,1)}, bf16[1,2,336,512]{3,2,1,0:T(8,128)(2,1)S(1)}, u32[]{:S(2)}, u32[]{:S(2)}) collective-permute-start(bf16[1,2,336,512]{3,2,1,0:T(8,128)(2,1)} %sum_blocks.4), channel_id=1, source_target_pairs={{0,2},{1,3},{2,0},{3,1},{4,6},{5,7},{6,4},{7,5},{8,10},{9,11},{10,... | collective-permute-start | bytes 2064392 | tf_op jit(solution)/shard_map/ppermute | solution.py:61
  240.5 30.0 %copy-start.7 = (bf16[2,4,144,384]{3,2,1,0:T(8,128)(2,1)}, bf16[2,4,144,384]{3,2,1,0:T(8,128)(2,1)S(1)}, u32[]{:S(2)}) copy-start(bf16[2,4,144,384]{3,2,1,0:T(8,128)(2,1)S(1)} %collective-permute-done.24.refs_11_) | copy-start | bytes 2654212
  240.5 30.0 %copy-start.8 = (bf16[2,4,144,384]{3,2,1,0:T(8,128)(2,1)}, bf16[2,4,144,384]{3,2,1,0:T(8,128)(2,1)S(1)}, u32[]{:S(2)}) copy-start(bf16[2,4,144,384]{3,2,1,0:T(8,128)(2,1)S(1)} %collective-permute-done.26.refs_10_) | copy-start | bytes 2654212
  242.0 11.3 %collective-permute-start.27 = (bf16[1,4,144,384]{3,2,1,0:T(8,128)(2,1)S(1)}, bf16[1,4,144,384]{3,2,1,0:T(8,128)(2,1)S(1)}, u32[]{:S(2)}, u32[]{:S(2)}) collective-permute-start(bf16[1,4,144,384]{3,2,1,0:T(8,128)(2,1)S(1)} %add_convert_fusion), channel_id=1, source_target_pairs={{0,4},{1,5},{2,6},{3,7},{4,0},{5,1},{6,2},{7,3},{8,12},{9,13},{10,... | collective-permute-start | bytes 1327112 | tf_op jit(solution)/shard_map/ppermute | solution.py:61
  253.3 23.1 %copy-start.15 = (bf16[1,4,144,384]{3,2,1,0:T(8,128)(2,1)}, bf16[1,4,144,384]{3,2,1,0:T(8,128)(2,1)S(1)}, u32[]{:S(2)}) copy-start(bf16[1,4,144,384]{3,2,1,0:T(8,128)(2,1)S(1)} %collective-permute-done.27.refs_12_) | copy-start | bytes 1327108
  254.5 16.0 %collective-permute-start.28 = (bf16[1,2,144,384]{3,2,1,0:T(8,128)(2,1)S(1)}, bf16[1,2,144,384]{3,2,1,0:T(8,128)(2,1)S(1)}, u32[]{:S(2)}, u32[]{:S(2)}) collective-permute-start(bf16[1,2,144,384]{3,2,1,0:T(8,128)(2,1)S(1)} %add_convert_fusion.1), channel_id=1, source_target_pairs={{0,2},{1,3},{2,0},{3,1},{4,6},{5,7},{6,4},{7,5},{8,10},{9,11},{10,... | collective-permute-start | bytes 663560 | tf_op jit(solution)/shard_map/ppermute | solution.py:61
  254.8 21.6 %collective-permute-start.30 = (bf16[1,1,336,512]{3,2,1,0:T(8,128)(2,1)}, bf16[1,1,336,512]{3,2,1,0:T(8,128)(2,1)S(1)}, u32[]{:S(2)}, u32[]{:S(2)}) collective-permute-start(bf16[1,1,336,512]{3,2,1,0:T(8,128)(2,1)} %sum_blocks.5), channel_id=1, source_target_pairs={{0,1},{1,0},{2,3},{3,2},{4,5},{5,4},{6,7},{7,6},{8,9},{9,8},{10,11... | collective-permute-start | bytes 1032200 | tf_op jit(solution)/shard_map/ppermute | solution.py:61
  270.5 5.9 %copy-start.17 = (bf16[1,2,144,384]{3,2,1,0:T(8,128)(2,1)}, bf16[1,2,144,384]{3,2,1,0:T(8,128)(2,1)S(1)}, u32[]{:S(2)}) copy-start(bf16[1,2,144,384]{3,2,1,0:T(8,128)(2,1)S(1)} %collective-permute-done.28.refs_13_) | copy-start | bytes 663556
  271.6 4.8 %collective-permute-start.29 = (bf16[1,1,144,384]{3,2,1,0:T(8,128)(2,1)S(1)}, bf16[1,1,144,384]{3,2,1,0:T(8,128)(2,1)S(1)}, u32[]{:S(2)}, u32[]{:S(2)}) collective-permute-start(bf16[1,1,144,384]{3,2,1,0:T(8,128)(2,1)S(1)} %add_convert_fusion.2), channel_id=1, source_target_pairs={{0,1},{1,0},{2,3},{3,2},{4,5},{5,4},{6,7},{7,6},{8,9},{9,8},{10,11... | collective-permute-start | bytes 331784 | tf_op jit(solution)/shard_map/ppermute | solution.py:61
  280.7 2.1 collective-permute-start.31
  (12 other events, 12.8 us)
